TPU v7x, 1024 devices: a whole 4x8x16 slice. The times are simulated.
1024 devices in a mesh: slab: 8 (over y), work: 128 (over z, x, core).
Axes of the slice: x: 4, y: 8, z: 16, core: 2. Of those that a mesh axis runs over, the one named last changes fastest.
Arguments:
- particles: float32 [8, 4096, 128], P(None, ('slab', 'work')), may hold values from -5 to 5, as said below
- counts: int32 [4096], P(('slab', 'work')), may hold values from 64 to 128
- partners: int32 [4096, 8], P(('slab', 'work')), may hold values from 0 to 511
Outputs:
- density: float32 [4096, 128], P(('slab', 'work'))
- acceleration: float32 [3, 4096, 128], P(None, ('slab', 'work'))
Inputs may be any that keep to these rules, and one draw needn't show every extreme that they name: `particles`: rows 0 to 2 hold positions in [0, 1], rows 3 to 5 velocities in [-5, 5], row 6 smoothing lengths in [0.6, 1.2], row 7 masses in [0.0005, 0.004]. Slots from counts[g] on are empty. `partners`: partner bins lie in the bin's own slab.
All inputs are finite; a program needn't handle non-finite values.
Results may differ from a plain program's by a relative error of at most 0.00005.
Values sent between devices are 32-bit elements; how exact they have to be, the bound alone decides.
No kernel may reach another device: no remote copies, remote signals or barrier semaphores. Data moves between devices by JAX's collectives and lax.ppermute only.
A program may use at most 32 MiB of HBM per device.

v0:
```python
import jax
import jax.numpy as jnp
from jax import lax
from jax.sharding import PartitionSpec as P

weight_norm = 21.0 / (16.0 * 3.141592653589793)
force_norm = 105.0 / (16.0 * 3.141592653589793)
viscosity = 0.25


def extended(shard, sides, width):
    for axis, dim in sides:
        count, length = (lax.axis_size(axis), shard.shape[dim])
        up = [(i, (i + 1) % count) for i in range(count)]
        down = [(j, i) for i, j in up]
        last = lax.slice_in_dim(shard, length - width, length, axis=dim)
        first = lax.slice_in_dim(shard, 0, width, axis=dim)
        before = lax.ppermute(last, axis, up)
        after = lax.ppermute(first, axis, down)
        shard = jnp.concatenate([before, shard, after], axis=dim)
    return shard


def separations(pos_self, pos_other):
    offset_vec = pos_self[:, :, None] - pos_other[:, None, :]
    radius = jnp.sqrt(jnp.sum(offset_vec * offset_vec, axis=0))
    return (offset_vec, radius)


def density_sum(pos_self, len_self, pos_other, mass_other):
    offset_vec, radius = separations(pos_self, pos_other)
    scaled = radius / len_self[:, None]
    shell_val = jnp.maximum(1.0 - 0.5 * scaled, 0.0)
    kernel = shell_val**4 * (1.0 + 2.0 * scaled) * (weight_norm / len_self**3)[:, None]
    return jnp.sum(kernel * mass_other[None, :], axis=1)


def force_sum(
    pos_self, vel_self, len_self, rho_self, pos_other, vel_other, len_other, mass_other, rho_other
):
    offset_vec, radius = separations(pos_self, pos_other)
    joint_h = 0.5 * (len_self[:, None] + len_other[None, :])
    scaled = radius / joint_h
    shell_val = jnp.maximum(1.0 - 0.5 * scaled, 0.0)
    factor = force_norm * shell_val**3 / joint_h**5 * mass_other[None, :]
    pressure = factor * (1.0 / rho_self[:, None] + 1.0 / rho_other[None, :])
    damping = factor * viscosity / (rho_self[:, None] * rho_other[None, :])
    veldiff = vel_self[:, :, None] - vel_other[:, None, :]
    return jnp.sum(pressure[None] * offset_vec - damping[None] * veldiff, axis=2)


def collect(link_ids, arrived):
    arrived_count = arrived.shape[1]
    offsets = jnp.arange(arrived_count, dtype=jnp.int32)
    chosen = (link_ids[:, None] == offsets[None, :]).astype(jnp.float32)
    return jnp.einsum("ln,cnp->clp", chosen, arrived, precision=lax.Precision.HIGHEST)


def density_bin(inputs):
    own_bin, gathered = inputs
    return density_sum(own_bin[0:3], own_bin[6], gathered[0:3], gathered[7])


def force_bin(inputs):
    own_bin, gathered = inputs
    return force_sum(
        own_bin[0:3],
        own_bin[3:6],
        own_bin[6],
        own_bin[8],
        gathered[0:3],
        gathered[3:6],
        gathered[6],
        gathered[7],
        gathered[8],
    )


def per_device(particles, counts, partners):
    channels, bin_count, slot_count = particles.shape
    link_count = partners.shape[1]
    slot_ids = jnp.arange(slot_count, dtype=jnp.int32)
    filled = (slot_ids[None, :] < counts[:, None]).astype(jnp.float32)
    masked = jnp.concatenate([particles[:7], particles[7:] * filled[None]], axis=0)
    link_ids = partners.reshape(-1)

    def gather_into(arrived):
        return collect(link_ids, arrived)

    def assemble(own_rows, rim_rows, far_rows, depth_rows):
        stacked = jnp.concatenate(
            [
                own_rows[:, :, None],
                rim_rows[0][:, :, None],
                rim_rows[2][:, :, None],
                far_rows.reshape(depth_rows, bin_count, link_count, slot_count),
            ],
            axis=2,
        )
        return jnp.transpose(stacked, (1, 0, 2, 3)).reshape(
            bin_count, depth_rows, (3 + link_count) * slot_count
        )

    rim_state = extended(masked[None], (("slab", 0),), 1)
    far_state = gather_into(lax.all_gather(masked, "work", axis=1, tiled=True))
    members = assemble(masked, rim_state, far_state, 8)
    owners = jnp.transpose(masked, (1, 0, 2))
    raw_density = lax.map(density_bin, (owners, members))
    safe_density = filled * raw_density + (1.0 - filled)
    density = filled * raw_density
    rim_rho = extended(safe_density[None, None], (("slab", 0),), 1)
    full_state = jnp.concatenate([masked, safe_density[None]], axis=0)
    far_full = gather_into(lax.all_gather(full_state, "work", axis=1, tiled=True))
    rim_full = jnp.concatenate([rim_state, rim_rho], axis=1)
    members_full = assemble(full_state, rim_full, far_full, 9)
    owners_full = jnp.transpose(full_state, (1, 0, 2))
    acceleration = lax.map(force_bin, (owners_full, members_full)) * filled[:, None, :]
    return (density, jnp.transpose(acceleration, (1, 0, 2)))


def solution(mesh):
    placed = (P(None, ("slab", "work"), None), P(("slab", "work")), P(("slab", "work"), None))
    return jax.shard_map(
        per_device,
        mesh=mesh,
        in_specs=placed,
        out_specs=(P(("slab", "work"), None), P(None, ("slab", "work"), None)),
        check_vma=False,
    )
```

profile of v0, /device:TPU:1, one launch (start us, length us, event | category | flops | bytes accessed | tf_op | source)
XLA Modules:
  0.0 341.5 jit_solution(16548907940329740049)
XLA Ops:
  7.2 0.7 slice.67
  7.9 0.7 slice.66
  8.6 0.7 compare_select_fusion
  10.0 5.9 %collective-permute-start.1 = (f32[1,8,4,128]{3,1,2,0:T(8,128)S(1)}, f32[1,8,4,128]{3,1,2,0:T(8,128)S(1)}, u32[]{:S(2)}, u32[]{:S(2)}) collective-permute-start(f32[1,8,4,128]{3,1,2,0:T(8,128)S(1)} %fusion.39), channel_id=1, source_target_pairs={{128,0},{256,128},{384,256},{512,384},{640,512},{768,640},{896,768... | collective-permute-start | bytes 49160 | tf_op jit(solution)/shard_map/ppermute | solution.py:19
  16.0 1.9 collective-permute-start
  17.9 0.8 eq.8
  18.8 2.9 collective-permute-done
  21.7 147.4 %all-gather.3.cloned.1.call-done = f32[8,512,128]{2,0,1:T(8,128)} async-done(((f32[8,4,128]{2,0,1:T(8,128)}), f32[8,512,128]{2,0,1:T(8,128)}) %all-gather.3.cloned.1.call-update) | async-done | bytes 2097168 | tf_op jit(solution)/shard_map/all_gather | solution.py:105
  169.0 2.6 fusion.21
  171.9 4.0 %while.22 = (s32[]{:T(128)}, f32[4,128]{1,0:T(4,128)S(1)}, f32[4,8,128]{2,1,0:T(8,128)S(1)}, f32[4,8,1408]{2,1,0:T(8,128)S(1)}) while((s32[]{:T(128)}, f32[4,128]{1,0:T(4,128)S(1)}, f32[4,8,128]{2,1,0:T(8,128)S(1)}, f32[4,8,1408]{2,1,0:T(8,128)S(1)}) %tuple.86), condition=%wide.region_3.4_spmd.clone, body=%wide.region_0.3_spmd.sunk.clone | while | flops 3604739 | bytes 1526877 | solution.py:108
  175.9 0.6 subtract_add_fusion
  177.2 4.5 %collective-permute-start.3 = (f32[1,1,4,128]{3,1,2,0:T(1,128)S(1)}, f32[1,1,4,128]{3,1,2,0:T(1,128)S(1)}, u32[]{:S(2)}, u32[]{:S(2)}) collective-permute-start(f32[1,1,4,128]{3,1,2,0:T(1,128)S(1)} %bitcast.115), channel_id=1, source_target_pairs={{128,0},{256,128},{384,256},{512,384},{640,512},{768,640},{896,768... | collective-permute-start | bytes 6152 | tf_op jit(solution)/shard_map/ppermute | solution.py:19
  181.6 1.9 collective-permute-start.2
  183.7 3.5 %collective-permute-done.2 = f32[1,1,4,128]{3,1,2,0:T(1,128)S(1)} collective-permute-done((f32[1,1,4,128]{3,1,2,0:T(1,128)S(1)}, f32[1,1,4,128]{3,1,2,0:T(1,128)S(1)}, u32[]{:S(2)}, u32[]{:S(2)}) %collective-permute-start.2) | collective-permute-done | bytes 2080 | tf_op jit(solution)/shard_map/ppermute | solution.py:18
  187.2 135.0 %all-gather.5.cloned.1.call-done = f32[9,512,128]{2,0,1:T(8,128)} async-done(((f32[9,4,128]{2,0,1:T(8,128)}), f32[9,512,128]{2,0,1:T(8,128)}) %all-gather.5.cloned.1.call-update) | async-done | bytes 2359312 | tf_op jit(solution)/shard_map/all_gather | solution.py:113
  322.2 3.7 %fusion.18 = f32[9,4,8,128]{3,2,1,0:T(8,128)S(1)} fusion(f32[9,512,128]{2,0,1:T(8,128)} %all-gather.5.cloned.1.call-done, s32[32]{0:T(128)S(1)} %eq.8), kind=kOutput, calls=%fused_computation.45 | convolution fusion | flops 226508800 | bytes 2506880 | tf_op jit(solution)/shard_map/ln,cnp->clp/dot_general | solution.py:56
  326.1 8.0 %while.23 = (s32[]{:T(128)}, f32[4,3,128]{2,0,1:T(4,128)S(1)}, f32[4,9,128]{2,1,0:T(8,128)S(1)}, f32[4,9,1408]{2,0,1:T(4,128)S(1)}) while((s32[]{:T(128)}, f32[4,3,128]{2,0,1:T(4,128)S(1)}, f32[4,9,128]{2,1,0:T(8,128)S(1)}, f32[4,9,1408]{2,0,1:T(4,128)S(1)}) %tuple.79), condition=%wide.region_7.8_spmd.clone, body=%wide.region_4.7_spmd.sunk.clone | while | flops 8111238 | bytes 6043297 | solution.py:117
  326.6 0.6 add_multiply_fusion.3
  327.4 0.6 fusion.58
  328.6 0.6 add_multiply_fusion.3
  329.4 0.6 fusion.58
  330.6 0.6 add_multiply_fusion.3
  331.4 0.6 fusion.58
  332.6 0.6 add_multiply_fusion.3
  (110 shorter events, 9.5 us)
Async XLA Ops:
  7.2 161.9 %all-gather.3.cloned.1.call-start = ((), (), s32[]{:S(2)}) async-start(), calls=%async_computation | async-start | bytes 2113536 | tf_op jit(solution)/shard_map/all_gather | solution.py:105
  10.0 312.3 %all-gather.5.cloned.1.call-start = ((), (), s32[]{:S(2)}) async-start(), calls=%async_computation.1 | async-start | bytes 4227072 | tf_op jit(solution)/shard_map/all_gather | solution.py:113
  10.0 8.7 %collective-permute-start.1 = (f32[1,8,4,128]{3,1,2,0:T(8,128)S(1)}, f32[1,8,4,128]{3,1,2,0:T(8,128)S(1)}, u32[]{:S(2)}, u32[]{:S(2)}) collective-permute-start(f32[1,8,4,128]{3,1,2,0:T(8,128)S(1)} %fusion.39), channel_id=1, source_target_pairs={{128,0},{256,128},{384,256},{512,384},{640,512},{768,640},{896,768... | collective-permute-start | bytes 49160 | tf_op jit(solution)/shard_map/ppermute | solution.py:19
  16.0 5.7 %collective-permute-start = (f32[1,8,4,128]{3,1,2,0:T(8,128)S(1)}, f32[1,8,4,128]{3,1,2,0:T(8,128)S(1)}, u32[]{:S(2)}, u32[]{:S(2)}) collective-permute-start(f32[1,8,4,128]{3,1,2,0:T(8,128)S(1)} %fusion.39), channel_id=1, source_target_pairs={{0,128},{128,256},{256,384},{384,512},{512,640},{640,768},{768,896... | collective-permute-start | bytes 49160 | tf_op jit(solution)/shard_map/ppermute | solution.py:18
  171.9 4.0 %copy-start = (s32[4]{0:T(128)S(1)}, s32[4]{0:T(128)}, u32[]{:S(2)}) copy-start(s32[4]{0:T(128)} %param.8) | copy-start | bytes 52
  177.2 6.5 %collective-permute-start.3 = (f32[1,1,4,128]{3,1,2,0:T(1,128)S(1)}, f32[1,1,4,128]{3,1,2,0:T(1,128)S(1)}, u32[]{:S(2)}, u32[]{:S(2)}) collective-permute-start(f32[1,1,4,128]{3,1,2,0:T(1,128)S(1)} %bitcast.115), channel_id=1, source_target_pairs={{128,0},{256,128},{384,256},{512,384},{640,512},{768,640},{896,768... | collective-permute-start | bytes 6152 | tf_op jit(solution)/shard_map/ppermute | solution.py:19
  181.6 5.5 %collective-permute-start.2 = (f32[1,1,4,128]{3,1,2,0:T(1,128)S(1)}, f32[1,1,4,128]{3,1,2,0:T(1,128)S(1)}, u32[]{:S(2)}, u32[]{:S(2)}) collective-permute-start(f32[1,1,4,128]{3,1,2,0:T(1,128)S(1)} %bitcast.116), channel_id=1, source_target_pairs={{0,128},{128,256},{256,384},{384,512},{512,640},{640,768},{768,896... | collective-permute-start | bytes 6152 | tf_op jit(solution)/shard_map/ppermute | solution.py:18
Sparse Core Ops, SparseCore 0:
  12.3 156.7 all-gather.2
  177.3 144.9 all-gather.4
where the time goes:
time: 342 us
  waiting for transfers between devices  289 us (85%)
  starting transfers between devices  14.3 us (4%)
  between operations  14.2 us (4%)
  other arithmetic  13.7 us (4%)
  matrix products  6.29 us (2%)
  local copies, waits for them, and re-layouts  3.58 us (1%)
    all_gather x1, waiting for transfers between devices, per_device(): far_state = gather_into(lax.all_gather(masked, 'work', axis=1, tiled=True))  147 us
    all_gather x1, waiting for transfers between devices, per_device(): lax.all_gather(full_state, 'work', axis=1, tiled=True)  135 us
    ppermute x2, starting transfers between devices, extended(): after = lax.ppermute(first, axis, down)  10.4 us
  transfers between devices with their start and end apart: 6, of which 4 were waited for; matrix products, arithmetic and copies ran while one was open for 0% of the time, Pallas kernels for 0%

commit v1 on v0

v1 whole, which is shorter than its diff:
```python
import jax
import jax.numpy as jnp
from jax import lax
from jax.experimental import pallas as pl
from jax.experimental.pallas import tpu as pltpu
from jax.sharding import Mesh, PartitionSpec as P

weight_norm = 21.0 / (16.0 * 3.141592653589793)
force_norm = 105.0 / (16.0 * 3.141592653589793)
viscosity = 0.25

BINS = 4
LINKS = 8
SLOTS = 128
ROWS = 8
COUNT = 3 + LINKS
VMEM = pltpu.MemorySpace.VMEM
SMEM = pltpu.MemorySpace.SMEM


def locate(bin_id):
    slot = bin_id & 3
    core = (bin_id >> 2) & 1
    col = (bin_id >> 3) & 3
    layer = bin_id >> 5
    return layer, col, core, slot


def spread(rows, target, index):
    for r in range(rows.shape[0]):
        target[index, r] = jnp.broadcast_to(rows[r : r + 1, :], (8, SLOTS))


def load_members(b, partners, own, up, down, near, far, me, wide):
    spread(own[b], wide, 0)
    spread(up[b], wide, 1)
    spread(down[b], wide, 2)
    for k in range(LINKS):
        layer, col, core, slot = locate(partners[b, k])
        index = (col * 16 + layer) * BINS + slot
        tile = jnp.where(core == me, near[index], far[index])
        spread(tile, wide, 3 + k)


def density_kernel(partners, counts, own, up, down, near, far, raw_out, den_out, rho_out, wide, tall, acc):
    me = lax.axis_index("core")

    def per_bin(b, carry):
        load_members(b, partners, own, up, down, near, far, me, wide)
        tall[...] = own[b].T

        def per_chunk(c, carry):
            start = pl.multiple_of(c * 8, 8)
            cols = tall[pl.ds(start, 8), :]
            xi, yi, zi, hi = (jnp.broadcast_to(cols[:, r : r + 1], (8, SLOTS)) for r in (0, 1, 2, 6))
            inv = 0.5 / hi
            total = jnp.zeros((8, SLOTS), jnp.float32)
            for j in range(COUNT):
                dx = xi - wide[j, 0]
                dy = yi - wide[j, 1]
                dz = zi - wide[j, 2]
                half = jnp.sqrt(dx * dx + dy * dy + dz * dz) * inv
                s = jnp.maximum(1.0 - half, 0.0)
                s2 = s * s
                total = total + (s2 * s2) * (1.0 + 4.0 * half) * wide[j, 7]
            acc[pl.ds(start, 8), :] = total * (weight_norm / (hi * hi * hi))
            return carry

        lax.fori_loop(0, SLOTS // 8, per_chunk, 0)
        raw = jnp.sum(acc[...].T, axis=0, keepdims=True)
        lane = lax.broadcasted_iota(jnp.int32, (1, SLOTS), 1)
        filled = (lane < counts[b]).astype(jnp.float32)
        den_out[pl.ds(b, 1), :] = filled * raw
        rho_out[pl.ds(b, 1), :] = filled * raw + (1.0 - filled)
        return carry

    lax.fori_loop(0, BINS, per_bin, 0)


def force_kernel(
    partners, counts, own, up, down, near, far, rho, rho_up, rho_down, rho_near, rho_far, out, wide, wide_rho, tall, tall_rho, acc
):
    me = lax.axis_index("core")

    def per_bin(b, carry):
        load_members(b, partners, own, up, down, near, far, me, wide)
        row = pl.ds(b, 1)
        for j, ref in enumerate((rho, rho_up, rho_down)):
            wide_rho[j] = jnp.broadcast_to(1.0 / ref[row, :], (8, SLOTS))
        for k in range(LINKS):
            layer, col, core, slot = locate(partners[b, k])
            at = pl.ds((layer * 4 + col) * BINS + slot, 1)
            value = jnp.where(core == me, rho_near[at, :], rho_far[at, :])
            wide_rho[3 + k] = jnp.broadcast_to(1.0 / value, (8, SLOTS))
        tall[...] = own[b].T
        tall_rho[...] = wide_rho[0].T

        def per_chunk(c, carry):
            start = pl.multiple_of(c * 8, 8)
            cols = tall[pl.ds(start, 8), :]
            xi, yi, zi, ui, vi, wi, hi = (jnp.broadcast_to(cols[:, r : r + 1], (8, SLOTS)) for r in range(7))
            di = jnp.broadcast_to(tall_rho[pl.ds(start, 8), :][:, 0:1], (8, SLOTS))
            drag = viscosity * di
            ax = jnp.zeros((8, SLOTS), jnp.float32)
            ay, az = ax, ax
            for j in range(COUNT):
                dx = xi - wide[j, 0]
                dy = yi - wide[j, 1]
                dz = zi - wide[j, 2]
                radius = jnp.sqrt(dx * dx + dy * dy + dz * dz)
                inv = 1.0 / (hi + wide[j, 6])
                s = jnp.maximum(1.0 - radius * inv, 0.0) * inv
                dj = wide_rho[j]
                factor = (s * s * s) * (inv * inv) * wide[j, 7]
                push = factor * (di + dj)
                damp = factor * dj * drag
                ax = ax + (push * dx - damp * (ui - wide[j, 3]))
                ay = ay + (push * dy - damp * (vi - wide[j, 4]))
                az = az + (push * dz - damp * (wi - wide[j, 5]))
            acc[0, pl.ds(start, 8), :] = ax
            acc[1, pl.ds(start, 8), :] = ay
            acc[2, pl.ds(start, 8), :] = az
            return carry

        lax.fori_loop(0, SLOTS // 8, per_chunk, 0)
        lane = lax.broadcasted_iota(jnp.int32, (1, SLOTS), 1)
        scale = (lane < counts[b]).astype(jnp.float32) * (32.0 * force_norm)
        for d in range(3):
            out[d, row, :] = jnp.sum(acc[d].T, axis=0, keepdims=True) * scale
        return carry

    lax.fori_loop(0, BINS, per_bin, 0)


def both_ways(value):
    count = lax.axis_size("slab")
    up = [(i, (i + 1) % count) for i in range(count)]
    down = [(j, i) for i, j in up]
    return lax.ppermute(value, "slab", up), lax.ppermute(value, "slab", down)


def exchange(block, axis):
    count = lax.axis_size(axis)
    return lax.all_to_all(jnp.broadcast_to(block[None], (count,) + block.shape), axis, 0, 0, tiled=True)


def other_core(value):
    return lax.ppermute(value, "core", [(0, 1), (1, 0)])


def per_device(particles, counts, partners):
    filled = (jnp.arange(SLOTS, dtype=jnp.int32)[None, :] < counts[:, None]).astype(jnp.float32)
    masked = jnp.concatenate([particles[:7], particles[7:] * filled[None]], axis=0)
    own = jnp.transpose(masked, (1, 0, 2))
    up, down = both_ways(own)
    column = exchange(own, "z")
    near = exchange(column, "x").reshape(-1, ROWS, SLOTS)
    far = other_core(near)
    f32 = jnp.float32
    smem, vmem = pl.BlockSpec(memory_space=SMEM), pl.BlockSpec(memory_space=VMEM)
    row_shape = jax.ShapeDtypeStruct((BINS, SLOTS), f32)
    density, rho = pl.pallas_call(
        lambda p, c, o, u, d, n, f, den, rh, *scratch: density_kernel(p, c, o, u, d, n, f, None, den, rh, *scratch),
        out_shape=(row_shape, row_shape),
        in_specs=[smem, smem] + [vmem] * 5,
        out_specs=(vmem, vmem),
        scratch_shapes=[
            pltpu.VMEM((COUNT, ROWS, 8, SLOTS), f32),
            pltpu.VMEM((SLOTS, ROWS), f32),
            pltpu.VMEM((SLOTS, SLOTS), f32),
        ],
        name="density",
    )(partners, counts, own, up, down, near, far)
    rho_up, rho_down = both_ways(rho)
    rho_near = exchange(rho, ("z", "x")).reshape(-1, SLOTS)
    rho_far = other_core(rho_near)
    acceleration = pl.pallas_call(
        force_kernel,
        out_shape=jax.ShapeDtypeStruct((3, BINS, SLOTS), f32),
        in_specs=[smem, smem] + [vmem] * 10,
        out_specs=vmem,
        scratch_shapes=[
            pltpu.VMEM((COUNT, ROWS, 8, SLOTS), f32),
            pltpu.VMEM((COUNT, 8, SLOTS), f32),
            pltpu.VMEM((SLOTS, ROWS), f32),
            pltpu.VMEM((SLOTS, 8), f32),
            pltpu.VMEM((3, SLOTS, SLOTS), f32),
        ],
        name="force",
    )(partners, counts, own, up, down, near, far, rho, rho_up, rho_down, rho_near, rho_far)
    return density, acceleration


def solution(mesh):
    grid = Mesh(mesh.devices.reshape(mesh.shape["slab"], 16, 4, 2), ("slab", "z", "x", "core"))
    axes = ("slab", "z", "x", "core")
    return jax.shard_map(
        per_device,
        mesh=grid,
        in_specs=(P(None, axes, None), P(axes), P(axes, None)),
        out_specs=(P(axes, None), P(None, axes, None)),
        check_vma=False,
    )
```

time: 342 us -> 134 us (0.39)
  waiting for transfers between devices: 289 us -> 5.9 us
  blocking collectives: 0 us -> 72.5 us
  Pallas kernels: 0 us -> 22.8 us
  other arithmetic: 13.7 us -> 0.08 us
  between operations: 14.2 us -> 0.8 us
  starting transfers between devices: 14.3 us -> 26.7 us
  matrix products: 6.29 us -> 0 us
    all_gather x2 -> x0, waiting for transfers between devices: 282 us -> none  [the longest x1 147 us: per_device(): far_state = gather_into(lax.all_gather(masked, 'work', axis=1, tiled=True))]
    all_to_all x0 -> x3, blocking collectives: none -> 72.5 us  [exchange(): lax.all_to_all(jnp.broadcast_to(block[None], (count,) + block.shape), axi...]
    pallas_call x0 -> x2, Pallas kernels: none -> 22.8 us  [the longest x1 12.5 us: per_device(): pl.pallas_call(force_kernel, out_shape=jax.ShapeDtypeStruct((3, BINS, SLO...]
    ppermute x4 -> x6, starting transfers between devices: 14.2 us -> 26.7 us  [the longest x2 14.4 us: other_core(): return lax.ppermute(value, 'core', [(0, 1), (1, 0)])]
    reduce_sum x16 -> x0, other arithmetic: 6.93 us -> none  [the longest x4 2.52 us: force_sum(): jnp.sum(pressure[None] * offset_vec - damping[None] * veldiff, axis=2)]
    dot_general x2 -> x0, matrix products: 6.29 us -> none  [collect(): jnp.einsum('ln,cnp->clp', chosen, arrived, precision=lax.Precision.HIGHEST)]
  transfers between devices with their start and end apart: 6 -> 6, of which waited for: 4 -> 2; matrix products, arithmetic and copies ran while one was open for 0% -> 0% of each run, Pallas kernels for 0% -> 0%
where the time goes in v1:
time: 134 us
  blocking collectives  72.5 us (54%)
  starting transfers between devices  26.7 us (20%)
  Pallas kernels  22.8 us (17%)
  waiting for transfers between devices  5.9 us (4%)
  local copies, waits for them, and re-layouts  5.01 us (4%)
    all_to_all x3, blocking collectives, exchange(): lax.all_to_all(jnp.broadcast_to(block[None], (count,) + block.shape), axi...  72.5 us
    ppermute x2, starting transfers between devices, other_core(): return lax.ppermute(value, 'core', [(0, 1), (1, 0)])  14.4 us
    pallas_call x1, Pallas kernels, per_device(): pl.pallas_call(force_kernel, out_shape=jax.ShapeDtypeStruct((3, BINS, SLO...  12.5 us
    ppermute x4, starting transfers between devices, both_ways(): return (lax.ppermute(value, 'slab', up), lax.ppermute(value, 'slab', down))  12.3 us
    pallas_call x1, Pallas kernels, per_device(): pl.pallas_call(lambda p, c, o, u, d, n, f, den, rh, *scratch: density_ker...  10.4 us
    ppermute x4, waiting for transfers between devices, both_ways(): return (lax.ppermute(value, 'slab', up), lax.ppermute(value, 'slab', down))  5.9 us
    unnamed x23, local copies, waits for them, and re-layouts  2.8 us
  transfers between devices with their start and end apart: 6, of which 2 were waited for; matrix products, arithmetic and copies ran while one was open for 0% of the time, Pallas kernels for 0%

profile of v1, /device:TPU:1, one launch (start us, length us, event | category | flops | bytes accessed | tf_op | source)
XLA Modules:
  0.0 133.8 jit_solution(9858049166484442134)
XLA Ops:
  0.6 0.7 slice-done.1
  1.4 0.7 slice-done
  2.0 0.1 compare_select_fusion
  2.1 33.0 %all_to_all.15 = f32[16,4,8,128]{3,2,1,0:T(8,128)S(1)} all-to-all(f32[16,4,8,128]{3,2,1,0:T(8,128)S(1)} %broadcast_in_dim.6), channel_id=1, replica_groups=mesh['slab'=8,'z'=16,'x'=4,'core'=2] {'z'}, dimensions={0} | all-to-all | bytes 524288 | tf_op jit(solution)/shard_map/all_to_all | solution.py:144
  35.1 0.1 broadcast_in_dim.7
  35.2 13.6 %all_to_all.16 = f32[4,16,4,8,128]{4,3,2,1,0:T(8,128)S(1)} all-to-all(f32[4,16,4,8,128]{4,3,2,1,0:T(8,128)S(1)} %broadcast_in_dim.7), channel_id=1, replica_groups=mesh['slab'=8,'z'=16,'x'=4,'core'=2] {'x'}, dimensions={0} | all-to-all | bytes 2097152 | tf_op jit(solution)/shard_map/all_to_all | solution.py:144
  48.8 8.9 %collective-permute-start.2 = (f32[256,8,128]{2,1,0:T(8,128)S(1)}, f32[256,8,128]{2,1,0:T(8,128)S(1)}, u32[]{:S(2)}, u32[]{:S(2)}) collective-permute-start(f32[256,8,128]{2,1,0:T(8,128)S(1)} %bitcast.5), channel_id=1, source_target_pairs={{0,1},{1,0},{2,3},{3,2},{4,5},{5,4},{6,7},{7,6},{8,9},{9,8},{10,11... | collective-permute-start | bytes 3145736 | tf_op jit(solution)/shard_map/ppermute | solution.py:148
  57.7 5.1 %collective-permute-start.1 = (f32[4,8,128]{2,1,0:T(8,128)S(1)}, f32[4,8,128]{2,1,0:T(8,128)S(1)}, u32[]{:S(2)}, u32[]{:S(2)}) collective-permute-start(f32[4,8,128]{2,1,0:T(8,128)S(1)} %maximum_bitcast_fusion.o.own), channel_id=1, source_target_pairs={{128,0},{256,128},{384,256},{512,384},{640,512},{768,640},{896,768... | collective-permute-start | bytes 49160 | tf_op jit(solution)/shard_map/ppermute | solution.py:139
  62.8 1.9 %collective-permute-start = (f32[4,8,128]{2,1,0:T(8,128)S(1)}, f32[4,8,128]{2,1,0:T(8,128)S(1)}, u32[]{:S(2)}, u32[]{:S(2)}) collective-permute-start(f32[4,8,128]{2,1,0:T(8,128)S(1)} %maximum_bitcast_fusion.o.own), channel_id=1, source_target_pairs={{0,128},{128,256},{256,384},{384,512},{512,640},{640,768},{768,896... | collective-permute-start | bytes 49160 | tf_op jit(solution)/shard_map/ppermute | solution.py:139
  64.8 0.0 collective-permute-done.1.d.down
  64.8 3.7 %collective-permute-done.u.up = f32[4,8,128]{2,1,0:T(8,128)S(1)} collective-permute-done((f32[4,8,128]{2,1,0:T(8,128)S(1)}, f32[4,8,128]{2,1,0:T(8,128)S(1)}, u32[]{:S(2)}, u32[]{:S(2)}) %collective-permute-start) | collective-permute-done | bytes 16416 | tf_op jit(solution)/shard_map/ppermute | solution.py:139
  68.5 0.0 collective-permute-done.2.f.far
  68.5 0.6 copy-done.6
  69.1 1.0 copy-done.1
  70.1 10.4 %density.1 = (f32[4,128]{1,0:T(4,128)}, f32[4,128]{1,0:T(4,128)}) custom-call(s32[4,8]{1,0:T(4,128)} %partners.1, s32[4]{0:T(128)} %counts.1, f32[4,8,128]{2,1,0:T(8,128)} %copy-done.3, f32[4,8,128]{2,1,0:T(8,128)} %copy-done.6, f32[4,8,128]{2,1,0:T(8,128)} %copy-done.5, f32[256,8,128]{2,1,0:T(8,128)} %bitcast.6, f32[256,8,128]{2,1,0:T(8,128)} %copy-done.1), custom_call_target="tpu_custom_call" | custom-call | tf_op jit(solution)/shard_map/density/pallas_call | solution.py:162
  80.5 0.7 broadcast_in_dim.8
  81.2 25.9 %all_to_all.17 = f32[64,4,128]{2,1,0:T(4,128)S(1)} all-to-all(f32[64,4,128]{2,1,0:T(4,128)S(1)} %broadcast_in_dim.8), channel_id=1, replica_groups=mesh['slab'=8,'z'=16,'x'=4,'core'=2] {'z','x'}, dimensions={0} | all-to-all | bytes 262144 | tf_op jit(solution)/shard_map/all_to_all | solution.py:144
  107.1 5.5 %collective-permute-start.5 = (f32[256,128]{1,0:T(8,128)S(1)}, f32[256,128]{1,0:T(8,128)S(1)}, u32[]{:S(2)}, u32[]{:S(2)}) collective-permute-start(f32[256,128]{1,0:T(8,128)S(1)} %bitcast.8), channel_id=1, source_target_pairs={{0,1},{1,0},{2,3},{3,2},{4,5},{5,4},{6,7},{7,6},{8,9},{9,8},{10,11... | collective-permute-start | bytes 393224 | tf_op jit(solution)/shard_map/ppermute | solution.py:148
  112.6 1.9 %collective-permute-start.4 = (f32[4,128]{1,0:T(4,128)S(1)}, f32[4,128]{1,0:T(4,128)S(1)}, u32[]{:S(2)}, u32[]{:S(2)}) collective-permute-start(f32[4,128]{1,0:T(4,128)S(1)} %copy-done.7), channel_id=1, source_target_pairs={{128,0},{256,128},{384,256},{512,384},{640,512},{768,640},{896,768... | collective-permute-start | bytes 6152 | tf_op jit(solution)/shard_map/ppermute | solution.py:139
  114.6 3.4 %collective-permute-start.3 = (f32[4,128]{1,0:T(4,128)S(1)}, f32[4,128]{1,0:T(4,128)S(1)}, u32[]{:S(2)}, u32[]{:S(2)}) collective-permute-start(f32[4,128]{1,0:T(4,128)S(1)} %copy-done.7), channel_id=1, source_target_pairs={{0,128},{128,256},{256,384},{384,512},{512,640},{640,768},{768,896... | collective-permute-start | bytes 6152 | tf_op jit(solution)/shard_map/ppermute | solution.py:139
  118.0 2.1 %collective-permute-done.3.rho_up = f32[4,128]{1,0:T(4,128)S(1)} collective-permute-done((f32[4,128]{1,0:T(4,128)S(1)}, f32[4,128]{1,0:T(4,128)S(1)}, u32[]{:S(2)}, u32[]{:S(2)}) %collective-permute-start.3) | collective-permute-done | bytes 2080 | tf_op jit(solution)/shard_map/ppermute | solution.py:139
  120.1 0.6 copy-done.10
  120.7 0.6 copy-done.4
  121.3 12.5 %force.1 = f32[3,4,128]{2,1,0:T(4,128)} custom-call(s32[4,8]{1,0:T(4,128)} %partners.1, s32[4]{0:T(128)} %counts.1, f32[4,8,128]{2,1,0:T(8,128)} %copy-done.3, f32[4,8,128]{2,1,0:T(8,128)} %copy-done.6, f32[4,8,128]{2,1,0:T(8,128)} %copy-done.5, f32[256,8,128]{2,1,0:T(8,128)} %bitcast.7, f32[256,8,128]{2,1,0:T(8,128)} %copy-done.1, ...), custom_call_target="tpu_custom_call" | custom-call | tf_op jit(solution)/shard_map/force/pallas_call | solution.py:177
  (25 shorter events, 0.1 us)
Async XLA Ops:
  0.6 0.7 slice-start.1
  1.3 0.7 slice-start
  1.3 0.7 copy-start.8
  2.1 60.7 %copy-start.3 = (f32[4,8,128]{2,1,0:T(8,128)}, f32[4,8,128]{2,1,0:T(8,128)S(1)}, u32[]{:S(2)}) copy-start(f32[4,8,128]{2,1,0:T(8,128)S(1)} %maximum_bitcast_fusion.o.own) | copy-start | bytes 49156
  48.8 19.7 %copy-start = (f32[4,16,4,8,128]{4,3,2,1,0:T(8,128)}, f32[4,16,4,8,128]{4,3,2,1,0:T(8,128)S(1)}, u32[]{:S(2)}) copy-start(f32[4,16,4,8,128]{4,3,2,1,0:T(8,128)S(1)} %all_to_all.16) | copy-start | bytes 3145732
  48.8 19.7 %collective-permute-start.2 = (f32[256,8,128]{2,1,0:T(8,128)S(1)}, f32[256,8,128]{2,1,0:T(8,128)S(1)}, u32[]{:S(2)}, u32[]{:S(2)}) collective-permute-start(f32[256,8,128]{2,1,0:T(8,128)S(1)} %bitcast.5), channel_id=1, source_target_pairs={{0,1},{1,0},{2,3},{3,2},{4,5},{5,4},{6,7},{7,6},{8,9},{9,8},{10,11... | collective-permute-start | bytes 3145736 | tf_op jit(solution)/shard_map/ppermute | solution.py:148
  57.7 7.0 %collective-permute-start.1 = (f32[4,8,128]{2,1,0:T(8,128)S(1)}, f32[4,8,128]{2,1,0:T(8,128)S(1)}, u32[]{:S(2)}, u32[]{:S(2)}) collective-permute-start(f32[4,8,128]{2,1,0:T(8,128)S(1)} %maximum_bitcast_fusion.o.own), channel_id=1, source_target_pairs={{128,0},{256,128},{384,256},{512,384},{640,512},{768,640},{896,768... | collective-permute-start | bytes 49160 | tf_op jit(solution)/shard_map/ppermute | solution.py:139
  62.8 5.7 %collective-permute-start = (f32[4,8,128]{2,1,0:T(8,128)S(1)}, f32[4,8,128]{2,1,0:T(8,128)S(1)}, u32[]{:S(2)}, u32[]{:S(2)}) collective-permute-start(f32[4,8,128]{2,1,0:T(8,128)S(1)} %maximum_bitcast_fusion.o.own), channel_id=1, source_target_pairs={{0,128},{128,256},{256,384},{384,512},{512,640},{640,768},{768,896... | collective-permute-start | bytes 49160 | tf_op jit(solution)/shard_map/ppermute | solution.py:139
  64.8 3.8 %copy-start.5 = (f32[4,8,128]{2,1,0:T(8,128)}, f32[4,8,128]{2,1,0:T(8,128)S(1)}, u32[]{:S(2)}) copy-start(f32[4,8,128]{2,1,0:T(8,128)S(1)} %collective-permute-done.1.d.down) | copy-start | bytes 49156
  68.5 0.6 copy-start.6
  69.1 1.0 copy-start.1
  81.2 31.5 %copy-start.7 = (f32[4,128]{1,0:T(4,128)S(1)}, f32[4,128]{1,0:T(4,128)}, u32[]{:S(2)}) copy-start(f32[4,128]{1,0:T(4,128)} %get-tuple-element.5.rho) | copy-start | bytes 6148
  107.1 13.0 %copy-start.2 = (f32[64,4,128]{2,1,0:T(4,128)}, f32[64,4,128]{2,1,0:T(4,128)S(1)}, u32[]{:S(2)}) copy-start(f32[64,4,128]{2,1,0:T(4,128)S(1)} %all_to_all.17) | copy-start | bytes 393220
  107.1 13.0 %collective-permute-start.5 = (f32[256,128]{1,0:T(8,128)S(1)}, f32[256,128]{1,0:T(8,128)S(1)}, u32[]{:S(2)}, u32[]{:S(2)}) collective-permute-start(f32[256,128]{1,0:T(8,128)S(1)} %bitcast.8), channel_id=1, source_target_pairs={{0,1},{1,0},{2,3},{3,2},{4,5},{5,4},{6,7},{7,6},{8,9},{9,8},{10,11... | collective-permute-start | bytes 393224 | tf_op jit(solution)/shard_map/ppermute | solution.py:148
  112.6 5.3 %collective-permute-start.4 = (f32[4,128]{1,0:T(4,128)S(1)}, f32[4,128]{1,0:T(4,128)S(1)}, u32[]{:S(2)}, u32[]{:S(2)}) collective-permute-start(f32[4,128]{1,0:T(4,128)S(1)} %copy-done.7), channel_id=1, source_target_pairs={{128,0},{256,128},{384,256},{512,384},{640,512},{768,640},{896,768... | collective-permute-start | bytes 6152 | tf_op jit(solution)/shard_map/ppermute | solution.py:139
  114.6 5.5 %collective-permute-start.3 = (f32[4,128]{1,0:T(4,128)S(1)}, f32[4,128]{1,0:T(4,128)S(1)}, u32[]{:S(2)}, u32[]{:S(2)}) collective-permute-start(f32[4,128]{1,0:T(4,128)S(1)} %copy-done.7), channel_id=1, source_target_pairs={{0,128},{128,256},{256,384},{384,512},{512,640},{640,768},{768,896... | collective-permute-start | bytes 6152 | tf_op jit(solution)/shard_map/ppermute | solution.py:139
  117.9 2.2 %copy-start.9 = (f32[4,128]{1,0:T(4,128)}, f32[4,128]{1,0:T(4,128)S(1)}, u32[]{:S(2)}) copy-start(f32[4,128]{1,0:T(4,128)S(1)} %collective-permute-done.4.rho_down) | copy-start | bytes 6148
  120.1 0.6 copy-start.10
  120.7 0.6 copy-start.4

commit v2 on v1

v2 whole, which is shorter than its diff:
```python
import jax
import jax.numpy as jnp
from jax import lax
from jax.experimental import pallas as pl
from jax.experimental.pallas import tpu as pltpu
from jax.sharding import Mesh, PartitionSpec as P

weight_norm = 21.0 / (16.0 * 3.141592653589793)
force_norm = 105.0 / (16.0 * 3.141592653589793)
viscosity = 0.25

BINS = 4
LINKS = 8
SLOTS = 128
ROWS = 8
COUNT = 3 + LINKS
CHUNKS = SLOTS // 8
F32 = jnp.float32
VMEM = pl.BlockSpec(memory_space=pltpu.MemorySpace.VMEM)
SMEM = pl.BlockSpec(memory_space=pltpu.MemorySpace.SMEM)
ANY = pl.BlockSpec(memory_space=pl.ANY)


def shape(*dims):
    return jax.ShapeDtypeStruct(dims, F32)


def root(square):
    return square * lax.rsqrt(jnp.maximum(square, 1e-36))


def columns(tall, c, rows):
    cols = tall[c * 8 : c * 8 + 8, :]
    return [jnp.broadcast_to(cols[:, r : r + 1], (8, SLOTS)) for r in rows]


def density_terms(tall, others, acc):
    for c in range(CHUNKS):
        xi, yi, zi, hi = columns(tall, c, (0, 1, 2, 6))
        inv = 0.5 / hi
        total = jnp.zeros((8, SLOTS), F32)
        for row in others:
            dx = xi - row(0)
            dy = yi - row(1)
            dz = zi - row(2)
            s = jnp.maximum(1.0 - root(dx * dx + dy * dy + dz * dz) * inv, 0.0)
            s2 = s * s
            total = total + (s2 * s2) * (5.0 - 4.0 * s) * row(7)
        acc[c * 8 : c * 8 + 8, :] = total * (weight_norm / (hi * hi * hi))
    return jnp.sum(acc[...].T, axis=0, keepdims=True)


def reader(ref, *index):
    return lambda r: ref[(*index, pl.ds(r, 8, stride=0), slice(None))]


def near_density_kernel(own, up, down, out, tall, acc):
    def per_bin(b, carry):
        tall[...] = own[b].T
        out[pl.ds(b, 1), :] = density_terms(tall, [reader(ref, b) for ref in (own, up, down)], acc)
        return carry

    lax.fori_loop(0, BINS, per_bin, 0)


def partner_density_kernel(partners, counts, own, part, near, far, den_out, inv_out, members, tall, acc, sems):
    me = lax.axis_index("core")

    def copies(b, k):
        bin_id = partners[b, k]
        index = (((bin_id >> 3) & 3) * 16 + (bin_id >> 5)) * BINS + (bin_id & 3)
        at = b * LINKS + k
        mine = ((bin_id >> 2) & 1) == me
        return mine, [pltpu.make_async_copy(ref.at[index], members.at[at], sems.at[at]) for ref in (near, far)]

    for b in range(BINS):
        for k in range(LINKS):
            mine, (from_near, from_far) = copies(b, k)
            pl.when(mine)(from_near.start)
            pl.when(jnp.logical_not(mine))(from_far.start)

    def per_bin(b, carry):
        tall[...] = own[b].T
        for k in range(LINKS):
            at = b * LINKS + k
            pltpu.make_async_copy(near.at[0], members.at[at], sems.at[at]).wait()
        far_part = density_terms(tall, [reader(members, b * LINKS + k) for k in range(LINKS)], acc)
        raw = part[pl.ds(b, 1), :] + far_part
        lane = lax.broadcasted_iota(jnp.int32, (1, SLOTS), 1)
        filled = (lane < counts[b]).astype(F32)
        den_out[pl.ds(b, 1), :] = filled * raw
        inv_out[pl.ds(b, 1), :] = 1.0 / (filled * raw + (1.0 - filled))
        return carry

    lax.fori_loop(0, BINS, per_bin, 0)


def factor_kernel(own, up, down, members, out, base, tall, acc):
    tall[...] = own[0].T
    others = [reader(ref, 0) for ref in (own, up, down)] + [reader(members, k) for k in range(LINKS)]
    for c in range(CHUNKS):
        xi, yi, zi, hi = columns(tall, c, (0, 1, 2, 6))
        ax = jnp.zeros((8, SLOTS), F32)
        ay, az = ax, ax
        for j, row in enumerate(others):
            dx = xi - row(0)
            dy = yi - row(1)
            dz = zi - row(2)
            inv = 1.0 / (hi + row(6))
            s = jnp.maximum(1.0 - root(dx * dx + dy * dy + dz * dz) * inv, 0.0) * inv
            factor = (s * s * s) * (inv * inv) * row(7)
            out[0, j, c * 8 : c * 8 + 8, :] = factor
            ax = ax + factor * dx
            ay = ay + factor * dy
            az = az + factor * dz
        for d, total in enumerate((ax, ay, az)):
            acc[d, c * 8 : c * 8 + 8, :] = total
    for d in range(3):
        base[0, d : d + 1, :] = jnp.sum(acc[d].T, axis=0, keepdims=True)


def force_kernel(partners, counts, own, up, down, members, factors, base, mine, mine_up, mine_down, inverse, out, weights, tall, acc):
    b = pl.program_id(0)
    for j, ref in enumerate((mine, mine_up, mine_down)):
        weights[j : j + 1, :] = ref[pl.ds(b, 1), :]
    for k in range(LINKS):
        weights[3 + k : 4 + k, :] = inverse[pl.ds(partners[b, k], 1), :]
    tall[...] = own[0].T
    others = [reader(ref, 0) for ref in (own, up, down)] + [reader(members, k) for k in range(LINKS)]
    for c in range(CHUNKS):
        xi, yi, zi, ui, vi, wi = columns(tall, c, range(6))
        ax = jnp.zeros((8, SLOTS), F32)
        ay, az, bx, by, bz = (ax,) * 5
        for j, row in enumerate(others):
            factor = factors[0, j, c * 8 : c * 8 + 8, :] * weights[pl.ds(j, 8, stride=0), :]
            ax = ax + factor * (xi - row(0))
            ay = ay + factor * (yi - row(1))
            az = az + factor * (zi - row(2))
            bx = bx + factor * (ui - row(3))
            by = by + factor * (vi - row(4))
            bz = bz + factor * (wi - row(5))
        for d, total in enumerate((ax, ay, az, bx, by, bz)):
            acc[d, c * 8 : c * 8 + 8, :] = total
    lane = lax.broadcasted_iota(jnp.int32, (1, SLOTS), 1)
    scale = (lane < counts[b]).astype(F32) * (32.0 * force_norm)
    weight = weights[0:1, :]
    for d in range(3):
        push = jnp.sum(acc[d].T, axis=0, keepdims=True)
        drag = jnp.sum(acc[3 + d].T, axis=0, keepdims=True)
        out[0, d : d + 1, :] = (push + weight * (base[0, d : d + 1, :] - viscosity * drag)) * scale


def both_ways(value):
    count = lax.axis_size("slab")
    up = [(i, (i + 1) % count) for i in range(count)]
    down = [(j, i) for i, j in up]
    return lax.ppermute(value, "slab", up), lax.ppermute(value, "slab", down)


def exchange(block, axis):
    count = lax.axis_size(axis)
    return lax.all_to_all(jnp.broadcast_to(block[None], (count,) + block.shape), axis, 0, 0, tiled=True)


def cost(pairs, ops):
    work = pairs * SLOTS * SLOTS
    return pl.CostEstimate(flops=work * ops, bytes_accessed=work * 4, transcendentals=work)


def limit(mib):
    return pltpu.CompilerParams(vmem_limit_bytes=mib << 20)


def per_device(particles, counts, partners):
    filled = (jnp.arange(SLOTS, dtype=jnp.int32)[None, :] < counts[:, None]).astype(F32)
    masked = jnp.concatenate([particles[:7], particles[7:] * filled[None]], axis=0)
    own = jnp.transpose(masked, (1, 0, 2))
    up, down = both_ways(own)
    column = exchange(own, "z")
    work_scratch = [pltpu.VMEM((SLOTS, ROWS), F32), pltpu.VMEM((SLOTS, SLOTS), F32)]
    part = pl.pallas_call(
        near_density_kernel,
        out_shape=shape(BINS, SLOTS),
        in_specs=[VMEM] * 3,
        out_specs=VMEM,
        scratch_shapes=work_scratch,
        cost_estimate=cost(3 * BINS, 20),
        compiler_params=limit(8),
        name="near_density",
    )(own, up, down)
    column, part = lax.optimization_barrier((column, part))
    near = exchange(column, "x").reshape(-1, ROWS, SLOTS)
    far = lax.ppermute(near, "core", [(0, 1), (1, 0)])
    density, mine, members = pl.pallas_call(
        partner_density_kernel,
        out_shape=(shape(BINS, SLOTS), shape(BINS, SLOTS), shape(BINS * LINKS, ROWS, SLOTS)),
        in_specs=[SMEM, SMEM, VMEM, VMEM, ANY, ANY],
        out_specs=(VMEM, VMEM, VMEM),
        scratch_shapes=work_scratch + [pltpu.SemaphoreType.DMA((BINS * LINKS,))],
        cost_estimate=cost(LINKS * BINS, 20),
        compiler_params=limit(8),
        name="partner_density",
    )(partners, counts, own, part, near, far)
    mine_up, mine_down = both_ways(mine)
    inverse = exchange(mine, ("z", "x", "core")).reshape(-1, SLOTS)
    tile = pl.BlockSpec((1, ROWS, SLOTS), lambda b: (b, 0, 0))
    links = pl.BlockSpec((LINKS, ROWS, SLOTS), lambda b: (b, 0, 0))
    pairs = pl.BlockSpec((1, COUNT, SLOTS, SLOTS), lambda b: (b, 0, 0, 0))
    vector = pl.BlockSpec((1, 3, SLOTS), lambda b: (b, 0, 0))
    factors, base = pl.pallas_call(
        factor_kernel,
        grid=(BINS,),
        out_shape=(shape(BINS, COUNT, SLOTS, SLOTS), shape(BINS, 3, SLOTS)),
        in_specs=[tile, tile, tile, links],
        out_specs=(pairs, vector),
        scratch_shapes=[pltpu.VMEM((SLOTS, ROWS), F32), pltpu.VMEM((3, SLOTS, SLOTS), F32)],
        cost_estimate=cost(COUNT * BINS, 40),
        compiler_params=limit(8),
        name="factor",
    )(own, up, down, members)
    acceleration = pl.pallas_call(
        force_kernel,
        grid=(BINS,),
        out_shape=shape(BINS, 3, SLOTS),
        in_specs=[SMEM, SMEM, tile, tile, tile, links, pairs, vector, VMEM, VMEM, VMEM, VMEM],
        out_specs=vector,
        scratch_shapes=[
            pltpu.VMEM((16, SLOTS), F32),
            pltpu.VMEM((SLOTS, ROWS), F32),
            pltpu.VMEM((6, SLOTS, SLOTS), F32),
        ],
        cost_estimate=cost(COUNT * BINS, 20),
        compiler_params=limit(8),
        name="force",
    )(partners, counts, own, up, down, members, factors, base, mine, mine_up, mine_down, inverse)
    return density, jnp.transpose(acceleration, (1, 0, 2))


def solution(mesh):
    grid = Mesh(mesh.devices.reshape(mesh.shape["slab"], 16, 4, 2), ("slab", "z", "x", "core"))
    axes = ("slab", "z", "x", "core")
    return jax.shard_map(
        per_device,
        mesh=grid,
        in_specs=(P(None, axes, None), P(axes), P(axes, None)),
        out_specs=(P(axes, None), P(None, axes, None)),
        check_vma=False,
    )
```

time: 134 us -> 105 us (0.78)
  blocking collectives: 72.5 us -> 13.6 us
  starting transfers between devices: 26.7 us -> 54.4 us
  waiting for transfers between devices: 5.9 us -> 17.2 us
  Pallas kernels: 22.8 us -> 13.3 us
  local copies, waits for them, and re-layouts: 5.01 us -> 3.61 us
    all_to_all x3 -> x1, blocking collectives: 72.5 us -> 13.6 us  [exchange(): lax.all_to_all(jnp.broadcast_to(block[None], (count,) + block.shape), axi...]
    all_to_all x0 -> x2, starting transfers between devices: none -> 31.5 us  [exchange(): lax.all_to_all(jnp.broadcast_to(block[None], (count,) + block.shape), axi...]
    all_to_all x0 -> x2, waiting for transfers between devices: none -> 10.7 us  [exchange(): lax.all_to_all(jnp.broadcast_to(block[None], (count,) + block.shape), axi...]
    pallas_call x2 -> x4, Pallas kernels: 22.8 us -> 13.3 us  [the longest x1 4.64 us: per_device(): pl.pallas_call(partner_density_kernel, out_shape=(shape(BINS, SLOTS), sha...]
    ppermute x2 -> x1, starting transfers between devices: 14.4 us -> 8.89 us  [per_device(): far = lax.ppermute(near, 'core', [(0, 1), (1, 0)])]
    ppermute x2 -> x1, waiting for transfers between devices: 0.01 us -> 2.26 us  [per_device(): far = lax.ppermute(near, 'core', [(0, 1), (1, 0)])]
    unnamed x23 -> x6, local copies, waits for them, and re-layouts: 2.8 us -> 0.61 us
    ppermute x4, starting transfers between devices: 12.3 us -> 14 us  [both_ways(): return (lax.ppermute(value, 'slab', up), lax.ppermute(value, 'slab', down))]
  transfers between devices with their start and end apart: 6 -> 7, of which waited for: 2 -> 5; matrix products, arithmetic and copies ran while one was open for 0% -> 0% of each run, Pallas kernels for 0% -> 5%
where the time goes in v2:
time: 105 us; the launch traced here: 104 us
  starting transfers between devices  54.4 us (52%)
  waiting for transfers between devices  17.2 us (16%)
  blocking collectives  13.6 us (13%)
  Pallas kernels  13.3 us (13%)
  local copies, waits for them, and re-layouts  3.61 us (3%)
    all_to_all x2, starting transfers between devices, exchange(): lax.all_to_all(jnp.broadcast_to(block[None], (count,) + block.shape), axi...  31.5 us
    ppermute x4, starting transfers between devices, both_ways(): return (lax.ppermute(value, 'slab', up), lax.ppermute(value, 'slab', down))  14 us
    all_to_all x1, blocking collectives, exchange(): lax.all_to_all(jnp.broadcast_to(block[None], (count,) + block.shape), axi...  13.6 us
    all_to_all x2, waiting for transfers between devices, exchange(): lax.all_to_all(jnp.broadcast_to(block[None], (count,) + block.shape), axi...  10.7 us
    ppermute x1, starting transfers between devices, per_device(): far = lax.ppermute(near, 'core', [(0, 1), (1, 0)])  8.89 us
    pallas_call x1, Pallas kernels, per_device(): pl.pallas_call(partner_density_kernel, out_shape=(shape(BINS, SLOTS), sha...  4.64 us
    ppermute x4, waiting for transfers between devices, both_ways(): return (lax.ppermute(value, 'slab', up), lax.ppermute(value, 'slab', down))  4.23 us
    pallas_call x1, Pallas kernels, per_device(): pl.pallas_call(factor_kernel, grid=(BINS,), out_shape=(shape(BINS, COUNT,...  3.71 us
  transfers between devices with their start and end apart: 7, of which 5 were waited for; matrix products, arithmetic and copies ran while one was open for 0% of the time, Pallas kernels for 5%

profile of v2, /device:TPU:1, one launch (start us, length us, event | category | flops | bytes accessed | tf_op | source)
XLA Modules:
  0.0 103.5 jit_solution(12374314909209806815)
XLA Ops:
  0.7 0.7 slice.7
  1.3 0.7 slice.6
  2.1 0.7 compare_select_fusion
  2.8 0.7 broadcast_in_dim.6
  3.5 19.4 %all-to-all-start = ((f32[16,4,8,128]{3,2,1,0:T(8,128)}), f32[16,4,8,128]{3,2,1,0:T(8,128)S(1)}, u32[]{:S(2)}, u32[]{:S(2)}) async-start(f32[16,4,8,128]{3,2,1,0:T(8,128)} %broadcast_in_dim.6), calls=%async_computation | async-start | bytes 524288 | tf_op jit(solution)/shard_map/all_to_all | solution.py:162
  22.9 5.1 %collective-permute-start.1 = (f32[4,8,128]{2,1,0:T(8,128)S(1)}, f32[4,8,128]{2,1,0:T(8,128)S(1)}, u32[]{:S(2)}, u32[]{:S(2)}) collective-permute-start(f32[4,8,128]{2,1,0:T(8,128)S(1)} %maximum_bitcast_fusion.own), channel_id=1, source_target_pairs={{128,0},{256,128},{384,256},{512,384},{640,512},{768,640},{896,768... | collective-permute-start | bytes 49160 | tf_op jit(solution)/shard_map/ppermute | solution.py:157
  28.1 1.9 %collective-permute-start = (f32[4,8,128]{2,1,0:T(8,128)S(1)}, f32[4,8,128]{2,1,0:T(8,128)S(1)}, u32[]{:S(2)}, u32[]{:S(2)}) collective-permute-start(f32[4,8,128]{2,1,0:T(8,128)S(1)} %maximum_bitcast_fusion.own), channel_id=1, source_target_pairs={{0,128},{128,256},{256,384},{384,512},{512,640},{640,768},{768,896... | collective-permute-start | bytes 49160 | tf_op jit(solution)/shard_map/ppermute | solution.py:157
  30.0 4.0 %collective-permute-done.up = f32[4,8,128]{2,1,0:T(8,128)S(1)} collective-permute-done((f32[4,8,128]{2,1,0:T(8,128)S(1)}, f32[4,8,128]{2,1,0:T(8,128)S(1)}, u32[]{:S(2)}, u32[]{:S(2)}) %collective-permute-start) | collective-permute-done | bytes 16416 | tf_op jit(solution)/shard_map/ppermute | solution.py:157
  34.0 1.5 %near_density.1.part = f32[4,128]{1,0:T(4,128)S(1)} custom-call(f32[4,8,128]{2,1,0:T(8,128)S(1)} %maximum_bitcast_fusion.own, f32[4,8,128]{2,1,0:T(8,128)S(1)} %collective-permute-done.up, f32[4,8,128]{2,1,0:T(8,128)S(1)} %collective-permute-done.1.down), custom_call_target="tpu_custom_call" | custom-call | flops 3932160 | bytes 786432 | tf_op jit(solution)/shard_map/near_density/pallas_call | solution.py:181
  35.6 1.1 %all-to-all-done = f32[16,4,8,128]{3,2,1,0:T(8,128)S(1)} async-done(((f32[16,4,8,128]{3,2,1,0:T(8,128)}), f32[16,4,8,128]{3,2,1,0:T(8,128)S(1)}, u32[]{:S(2)}, u32[]{:S(2)}) %all-to-all-start) | async-done | bytes 262176 | tf_op jit(solution)/shard_map/all_to_all | solution.py:162
  36.7 0.1 broadcast_in_dim.7
  36.8 13.6 %all_to_all.15 = f32[4,16,4,8,128]{4,3,2,1,0:T(8,128)S(1)} all-to-all(f32[4,16,4,8,128]{4,3,2,1,0:T(8,128)S(1)} %broadcast_in_dim.7), channel_id=1, replica_groups=mesh['slab'=8,'z'=16,'x'=4,'core'=2] {'x'}, dimensions={0} | all-to-all | bytes 2097152 | tf_op jit(solution)/shard_map/all_to_all | solution.py:162
  50.4 8.9 %collective-permute-start.2 = (f32[256,8,128]{2,1,0:T(8,128)S(1)}, f32[256,8,128]{2,1,0:T(8,128)S(1)}, u32[]{:S(2)}, u32[]{:S(2)}) collective-permute-start(f32[256,8,128]{2,1,0:T(8,128)S(1)} %bitcast.6), channel_id=1, source_target_pairs={{0,1},{1,0},{2,3},{3,2},{4,5},{5,4},{6,7},{7,6},{8,9},{9,8},{10,11... | collective-permute-start | bytes 3145736 | tf_op jit(solution)/shard_map/ppermute | solution.py:193
  59.3 2.3 %collective-permute-done.2.far = f32[256,8,128]{2,1,0:T(8,128)S(1)} collective-permute-done((f32[256,8,128]{2,1,0:T(8,128)S(1)}, f32[256,8,128]{2,1,0:T(8,128)S(1)}, u32[]{:S(2)}, u32[]{:S(2)}) %collective-permute-start.2) | collective-permute-done | bytes 1048608 | tf_op jit(solution)/shard_map/ppermute | solution.py:193
  61.6 4.6 %partner_density.1 = (f32[4,128]{1,0:T(4,128)}, f32[4,128]{1,0:T(4,128)S(1)}, f32[32,8,128]{2,1,0:T(8,128)S(1)}) custom-call(s32[4,8]{1,0:T(4,128)S(1)} %copy-done, s32[4]{0:T(128)S(1)} %copy-done.1, f32[4,8,128]{2,1,0:T(8,128)S(1)} %maximum_bitcast_fusion.own, f32[4,128]{1,0:T(4,128)S(1)} %near_density.1.part, f32[256,8,128]{2,1,0:T(8,128)S(1)} %bitcast.7, ...), custom_call_target="tpu_custom_call" | custom-call | flops 10485760 | bytes 2097152 | tf_op jit(solution)/shard_map/partner_density/pallas_call | solution.py:194
  66.2 0.7 broadcast_in_dim.8
  67.0 12.1 %all-to-all-start.2 = ((f32[128,4,128]{2,1,0:T(4,128)}), f32[128,4,128]{2,1,0:T(4,128)S(1)}, u32[]{:S(2)}, u32[]{:S(2)}) async-start(f32[128,4,128]{2,1,0:T(4,128)} %broadcast_in_dim.8), calls=%async_computation.2 | async-start | bytes 524288 | tf_op jit(solution)/shard_map/all_to_all | solution.py:162
  79.1 5.1 %collective-permute-start.4 = (f32[4,128]{1,0:T(4,128)S(1)}, f32[4,128]{1,0:T(4,128)S(1)}, u32[]{:S(2)}, u32[]{:S(2)}) collective-permute-start(f32[4,128]{1,0:T(4,128)S(1)} %get-tuple-element.15.mine), channel_id=1, source_target_pairs={{128,0},{256,128},{384,256},{512,384},{640,512},{768,640},{896,768... | collective-permute-start | bytes 6152 | tf_op jit(solution)/shard_map/ppermute | solution.py:157
  84.2 1.9 %collective-permute-start.3 = (f32[4,128]{1,0:T(4,128)S(1)}, f32[4,128]{1,0:T(4,128)S(1)}, u32[]{:S(2)}, u32[]{:S(2)}) collective-permute-start(f32[4,128]{1,0:T(4,128)S(1)} %get-tuple-element.15.mine), channel_id=1, source_target_pairs={{0,128},{128,256},{256,384},{384,512},{512,640},{640,768},{768,896... | collective-permute-start | bytes 6152 | tf_op jit(solution)/shard_map/ppermute | solution.py:157
  86.1 3.7 %factor.1 = (f32[4,11,128,128]{3,2,1,0:T(8,128)S(1)}, f32[4,3,128]{2,1,0:T(4,128)S(1)}) custom-call(f32[4,8,128]{2,1,0:T(8,128)S(1)} %maximum_bitcast_fusion.own, f32[4,8,128]{2,1,0:T(8,128)S(1)} %collective-permute-done.up, f32[4,8,128]{2,1,0:T(8,128)S(1)} %collective-permute-done.1.down, f32[32,8,128]{2,1,0:T(8,128)S(1)} %get-tuple-element.12.members), custom_call_target="tpu_custom_call" | custom-call | flops 28835840 | bytes 2883584 | tf_op jit(solution)/shard_map/factor/pallas_call | solution.py:210
  89.8 0.2 collective-permute-done.3.mine_up
  90.0 9.5 %all-to-all-done.2 = f32[128,4,128]{2,1,0:T(4,128)S(1)} async-done(((f32[128,4,128]{2,1,0:T(4,128)}), f32[128,4,128]{2,1,0:T(4,128)S(1)}, u32[]{:S(2)}, u32[]{:S(2)}) %all-to-all-start.2) | async-done | bytes 262176 | tf_op jit(solution)/shard_map/all_to_all | solution.py:162
  99.6 3.4 %force.1 = f32[4,3,128]{2,1,0:T(4,128)S(1)} custom-call(s32[4,8]{1,0:T(4,128)S(1)} %copy-done, s32[4]{0:T(128)S(1)} %copy-done.1, f32[4,8,128]{2,1,0:T(8,128)S(1)} %maximum_bitcast_fusion.own, f32[4,8,128]{2,1,0:T(8,128)S(1)} %collective-permute-done.up, f32[4,8,128]{2,1,0:T(8,128)S(1)} %collective-permute-done.1.down, ...), custom_call_target="tpu_custom_call" | custom-call | flops 14417920 | bytes 2883584 | tf_op jit(solution)/shard_map/force/pallas_call | solution.py:221
  102.9 0.6 copy.7
  (8 shorter events, 0.0 us)
Async XLA Ops:
  0.6 60.9 %copy-start.1 = (s32[4]{0:T(128)S(1)}, s32[4]{0:T(128)}, u32[]{:S(2)}) copy-start(s32[4]{0:T(128)} %counts.3) | copy-start | bytes 52
  0.6 60.9 %copy-start = (s32[4,8]{1,0:T(4,128)S(1)}, s32[4,8]{1,0:T(4,128)}, u32[]{:S(2)}) copy-start(s32[4,8]{1,0:T(4,128)} %partners.3) | copy-start | bytes 388
  3.5 33.2 %all-to-all-start = ((f32[16,4,8,128]{3,2,1,0:T(8,128)}), f32[16,4,8,128]{3,2,1,0:T(8,128)S(1)}, u32[]{:S(2)}, u32[]{:S(2)}) async-start(f32[16,4,8,128]{3,2,1,0:T(8,128)} %broadcast_in_dim.6), calls=%async_computation | async-start | bytes 524288 | tf_op jit(solution)/shard_map/all_to_all | solution.py:162
  22.9 7.0 %collective-permute-start.1 = (f32[4,8,128]{2,1,0:T(8,128)S(1)}, f32[4,8,128]{2,1,0:T(8,128)S(1)}, u32[]{:S(2)}, u32[]{:S(2)}) collective-permute-start(f32[4,8,128]{2,1,0:T(8,128)S(1)} %maximum_bitcast_fusion.own), channel_id=1, source_target_pairs={{128,0},{256,128},{384,256},{512,384},{640,512},{768,640},{896,768... | collective-permute-start | bytes 49160 | tf_op jit(solution)/shard_map/ppermute | solution.py:157
  28.1 6.0 %collective-permute-start = (f32[4,8,128]{2,1,0:T(8,128)S(1)}, f32[4,8,128]{2,1,0:T(8,128)S(1)}, u32[]{:S(2)}, u32[]{:S(2)}) collective-permute-start(f32[4,8,128]{2,1,0:T(8,128)S(1)} %maximum_bitcast_fusion.own), channel_id=1, source_target_pairs={{0,128},{128,256},{256,384},{384,512},{512,640},{640,768},{768,896... | collective-permute-start | bytes 49160 | tf_op jit(solution)/shard_map/ppermute | solution.py:157
  50.4 11.2 %collective-permute-start.2 = (f32[256,8,128]{2,1,0:T(8,128)S(1)}, f32[256,8,128]{2,1,0:T(8,128)S(1)}, u32[]{:S(2)}, u32[]{:S(2)}) collective-permute-start(f32[256,8,128]{2,1,0:T(8,128)S(1)} %bitcast.6), channel_id=1, source_target_pairs={{0,1},{1,0},{2,3},{3,2},{4,5},{5,4},{6,7},{7,6},{8,9},{9,8},{10,11... | collective-permute-start | bytes 3145736 | tf_op jit(solution)/shard_map/ppermute | solution.py:193
  67.0 32.6 %all-to-all-start.2 = ((f32[128,4,128]{2,1,0:T(4,128)}), f32[128,4,128]{2,1,0:T(4,128)S(1)}, u32[]{:S(2)}, u32[]{:S(2)}) async-start(f32[128,4,128]{2,1,0:T(4,128)} %broadcast_in_dim.8), calls=%async_computation.2 | async-start | bytes 524288 | tf_op jit(solution)/shard_map/all_to_all | solution.py:162
  79.1 10.7 %collective-permute-start.4 = (f32[4,128]{1,0:T(4,128)S(1)}, f32[4,128]{1,0:T(4,128)S(1)}, u32[]{:S(2)}, u32[]{:S(2)}) collective-permute-start(f32[4,128]{1,0:T(4,128)S(1)} %get-tuple-element.15.mine), channel_id=1, source_target_pairs={{128,0},{256,128},{384,256},{512,384},{640,512},{768,640},{896,768... | collective-permute-start | bytes 6152 | tf_op jit(solution)/shard_map/ppermute | solution.py:157
  84.2 5.8 %collective-permute-start.3 = (f32[4,128]{1,0:T(4,128)S(1)}, f32[4,128]{1,0:T(4,128)S(1)}, u32[]{:S(2)}, u32[]{:S(2)}) collective-permute-start(f32[4,128]{1,0:T(4,128)S(1)} %get-tuple-element.15.mine), channel_id=1, source_target_pairs={{0,128},{128,256},{256,384},{384,512},{512,640},{640,768},{768,896... | collective-permute-start | bytes 6152 | tf_op jit(solution)/shard_map/ppermute | solution.py:157

commit v3 on v2

--- a/solution.py
+++ b/solution.py
@@ -124,7 +124,9 @@
     for j, ref in enumerate((mine, mine_up, mine_down)):
         weights[j : j + 1, :] = ref[pl.ds(b, 1), :]
     for k in range(LINKS):
-        weights[3 + k : 4 + k, :] = inverse[pl.ds(partners[b, k], 1), :]
+        bin_id = partners[b, k]
+        at = (((bin_id >> 2) & 7) * 16 + (bin_id >> 5)) * BINS + (bin_id & 3)
+        weights[3 + k : 4 + k, :] = inverse[pl.ds(at, 1), :]
     tall[...] = own[0].T
     others = [reader(ref, 0) for ref in (own, up, down)] + [reader(members, k) for k in range(LINKS)]
     for c in range(CHUNKS):
@@ -202,7 +204,7 @@
         name="partner_density",
     )(partners, counts, own, part, near, far)
     mine_up, mine_down = both_ways(mine)
-    inverse = exchange(mine, ("z", "x", "core")).reshape(-1, SLOTS)
+    layer = exchange(mine, "z")
     tile = pl.BlockSpec((1, ROWS, SLOTS), lambda b: (b, 0, 0))
     links = pl.BlockSpec((LINKS, ROWS, SLOTS), lambda b: (b, 0, 0))
     pairs = pl.BlockSpec((1, COUNT, SLOTS, SLOTS), lambda b: (b, 0, 0, 0))
@@ -218,6 +220,8 @@
         compiler_params=limit(8),
         name="factor",
     )(own, up, down, members)
+    layer, base, mine_up, mine_down = lax.optimization_barrier((layer, base, mine_up, mine_down))
+    inverse = exchange(layer, ("x", "core")).reshape(-1, SLOTS)
     acceleration = pl.pallas_call(
         force_kernel,
         grid=(BINS,),

time: 105 us -> 103 us (0.981); the launches traced: 104 us -> 103 us
  blocking collectives: 13.6 us -> 24.2 us
  waiting for transfers between devices: 17.2 us -> 8.18 us
  starting transfers between devices: 54.4 us -> 52 us
    all_to_all x1 -> x2, blocking collectives: 13.6 us -> 24.2 us  [exchange(): lax.all_to_all(jnp.broadcast_to(block[None], (count,) + block.shape), axi...]
    all_to_all x2, waiting for transfers between devices: 10.7 us -> 1.68 us  [exchange(): lax.all_to_all(jnp.broadcast_to(block[None], (count,) + block.shape), axi...]
    all_to_all x2, starting transfers between devices: 31.5 us -> 29.1 us  [exchange(): lax.all_to_all(jnp.broadcast_to(block[None], (count,) + block.shape), axi...]
where the time goes in v3:
time: 103 us
  starting transfers between devices  52 us (50%)
  blocking collectives  24.2 us (23%)
  Pallas kernels  13.3 us (13%)
  waiting for transfers between devices  8.18 us (8%)
  local copies, waits for them, and re-layouts  3.52 us (3%)
    all_to_all x2, starting transfers between devices, exchange(): lax.all_to_all(jnp.broadcast_to(block[None], (count,) + block.shape), axi...  29.1 us
    all_to_all x2, blocking collectives, exchange(): lax.all_to_all(jnp.broadcast_to(block[None], (count,) + block.shape), axi...  24.2 us
    ppermute x4, starting transfers between devices, both_ways(): return (lax.ppermute(value, 'slab', up), lax.ppermute(value, 'slab', down))  14 us
    ppermute x1, starting transfers between devices, per_device(): far = lax.ppermute(near, 'core', [(0, 1), (1, 0)])  8.89 us
    pallas_call x1, Pallas kernels, per_device(): pl.pallas_call(partner_density_kernel, out_shape=(shape(BINS, SLOTS), sha...  4.64 us
    ppermute x4, waiting for transfers between devices, both_ways(): return (lax.ppermute(value, 'slab', up), lax.ppermute(value, 'slab', down))  4.23 us
    pallas_call x1, Pallas kernels, per_device(): pl.pallas_call(factor_kernel, grid=(BINS,), out_shape=(shape(BINS, COUNT,...  3.71 us
    pallas_call x1, Pallas kernels, per_device(): pl.pallas_call(force_kernel, grid=(BINS,), out_shape=shape(BINS, 3, SLOTS...  3.38 us
  transfers between devices with their start and end apart: 7, of which 5 were waited for; matrix products, arithmetic and copies ran while one was open for 0% of the time, Pallas kernels for 5%

profile of v3, /device:TPU:1, one launch (start us, length us, event | category | flops | bytes accessed | tf_op | source)
XLA Modules:
  0.0 102.6 jit_solution(8041628759989702161)
XLA Ops:
  0.7 0.7 slice.7
  1.3 0.7 slice.6
  2.1 0.7 compare_select_fusion
  2.8 0.7 broadcast_in_dim.8
  3.5 19.4 %all-to-all-start = ((f32[16,4,8,128]{3,2,1,0:T(8,128)}), f32[16,4,8,128]{3,2,1,0:T(8,128)S(1)}, u32[]{:S(2)}, u32[]{:S(2)}) async-start(f32[16,4,8,128]{3,2,1,0:T(8,128)} %broadcast_in_dim.8), calls=%async_computation | async-start | bytes 524288 | tf_op jit(solution)/shard_map/all_to_all | solution.py:164
  22.9 5.1 %collective-permute-start.1 = (f32[4,8,128]{2,1,0:T(8,128)S(1)}, f32[4,8,128]{2,1,0:T(8,128)S(1)}, u32[]{:S(2)}, u32[]{:S(2)}) collective-permute-start(f32[4,8,128]{2,1,0:T(8,128)S(1)} %maximum_bitcast_fusion.own), channel_id=1, source_target_pairs={{128,0},{256,128},{384,256},{512,384},{640,512},{768,640},{896,768... | collective-permute-start | bytes 49160 | tf_op jit(solution)/shard_map/ppermute | solution.py:159
  28.1 1.9 %collective-permute-start = (f32[4,8,128]{2,1,0:T(8,128)S(1)}, f32[4,8,128]{2,1,0:T(8,128)S(1)}, u32[]{:S(2)}, u32[]{:S(2)}) collective-permute-start(f32[4,8,128]{2,1,0:T(8,128)S(1)} %maximum_bitcast_fusion.own), channel_id=1, source_target_pairs={{0,128},{128,256},{256,384},{384,512},{512,640},{640,768},{768,896... | collective-permute-start | bytes 49160 | tf_op jit(solution)/shard_map/ppermute | solution.py:159
  30.0 4.0 %collective-permute-done.up = f32[4,8,128]{2,1,0:T(8,128)S(1)} collective-permute-done((f32[4,8,128]{2,1,0:T(8,128)S(1)}, f32[4,8,128]{2,1,0:T(8,128)S(1)}, u32[]{:S(2)}, u32[]{:S(2)}) %collective-permute-start) | collective-permute-done | bytes 16416 | tf_op jit(solution)/shard_map/ppermute | solution.py:159
  34.0 1.5 %near_density.1.part = f32[4,128]{1,0:T(4,128)S(1)} custom-call(f32[4,8,128]{2,1,0:T(8,128)S(1)} %maximum_bitcast_fusion.own, f32[4,8,128]{2,1,0:T(8,128)S(1)} %collective-permute-done.up, f32[4,8,128]{2,1,0:T(8,128)S(1)} %collective-permute-done.1.down), custom_call_target="tpu_custom_call" | custom-call | flops 3932160 | bytes 786432 | tf_op jit(solution)/shard_map/near_density/pallas_call | solution.py:183
  35.6 1.1 %all-to-all-done = f32[16,4,8,128]{3,2,1,0:T(8,128)S(1)} async-done(((f32[16,4,8,128]{3,2,1,0:T(8,128)}), f32[16,4,8,128]{3,2,1,0:T(8,128)S(1)}, u32[]{:S(2)}, u32[]{:S(2)}) %all-to-all-start) | async-done | bytes 262176 | tf_op jit(solution)/shard_map/all_to_all | solution.py:164
  36.8 13.6 %all_to_all.20 = f32[4,16,4,8,128]{4,3,2,1,0:T(8,128)S(1)} all-to-all(f32[4,16,4,8,128]{4,3,2,1,0:T(8,128)S(1)} %broadcast_in_dim.9), channel_id=1, replica_groups=mesh['slab'=8,'z'=16,'x'=4,'core'=2] {'x'}, dimensions={0} | all-to-all | bytes 2097152 | tf_op jit(solution)/shard_map/all_to_all | solution.py:164
  50.4 8.9 %collective-permute-start.2 = (f32[256,8,128]{2,1,0:T(8,128)S(1)}, f32[256,8,128]{2,1,0:T(8,128)S(1)}, u32[]{:S(2)}, u32[]{:S(2)}) collective-permute-start(f32[256,8,128]{2,1,0:T(8,128)S(1)} %bitcast.6), channel_id=1, source_target_pairs={{0,1},{1,0},{2,3},{3,2},{4,5},{5,4},{6,7},{7,6},{8,9},{9,8},{10,11... | collective-permute-start | bytes 3145736 | tf_op jit(solution)/shard_map/ppermute | solution.py:195
  59.3 2.3 %collective-permute-done.2.far = f32[256,8,128]{2,1,0:T(8,128)S(1)} collective-permute-done((f32[256,8,128]{2,1,0:T(8,128)S(1)}, f32[256,8,128]{2,1,0:T(8,128)S(1)}, u32[]{:S(2)}, u32[]{:S(2)}) %collective-permute-start.2) | collective-permute-done | bytes 1048608 | tf_op jit(solution)/shard_map/ppermute | solution.py:195
  61.6 4.6 %partner_density.1 = (f32[4,128]{1,0:T(4,128)}, f32[4,128]{1,0:T(4,128)S(1)}, f32[32,8,128]{2,1,0:T(8,128)S(1)}) custom-call(s32[4,8]{1,0:T(4,128)S(1)} %copy-done, s32[4]{0:T(128)S(1)} %copy-done.1, f32[4,8,128]{2,1,0:T(8,128)S(1)} %maximum_bitcast_fusion.own, f32[4,128]{1,0:T(4,128)S(1)} %near_density.1.part, f32[256,8,128]{2,1,0:T(8,128)S(1)} %bitcast.7, ...), custom_call_target="tpu_custom_call" | custom-call | flops 10485760 | bytes 2097152 | tf_op jit(solution)/shard_map/partner_density/pallas_call | solution.py:196
  66.2 0.6 broadcast_in_dim.10
  66.8 9.7 %all-to-all-start.2 = ((f32[16,4,128]{2,1,0:T(4,128)}), f32[16,4,128]{2,1,0:T(4,128)S(1)}, u32[]{:S(2)}, u32[]{:S(2)}) async-start(f32[16,4,128]{2,1,0:T(4,128)} %broadcast_in_dim.10), calls=%async_computation.2 | async-start | bytes 65536 | tf_op jit(solution)/shard_map/all_to_all | solution.py:164
  76.5 5.1 %collective-permute-start.4 = (f32[4,128]{1,0:T(4,128)S(1)}, f32[4,128]{1,0:T(4,128)S(1)}, u32[]{:S(2)}, u32[]{:S(2)}) collective-permute-start(f32[4,128]{1,0:T(4,128)S(1)} %get-tuple-element.18.mine), channel_id=1, source_target_pairs={{128,0},{256,128},{384,256},{512,384},{640,512},{768,640},{896,768... | collective-permute-start | bytes 6152 | tf_op jit(solution)/shard_map/ppermute | solution.py:159
  81.6 1.9 %collective-permute-start.3 = (f32[4,128]{1,0:T(4,128)S(1)}, f32[4,128]{1,0:T(4,128)S(1)}, u32[]{:S(2)}, u32[]{:S(2)}) collective-permute-start(f32[4,128]{1,0:T(4,128)S(1)} %get-tuple-element.18.mine), channel_id=1, source_target_pairs={{0,128},{128,256},{256,384},{384,512},{512,640},{640,768},{768,896... | collective-permute-start | bytes 6152 | tf_op jit(solution)/shard_map/ppermute | solution.py:159
  83.5 3.7 %factor.1 = (f32[4,11,128,128]{3,2,1,0:T(8,128)S(1)}, f32[4,3,128]{2,1,0:T(4,128)S(1)}) custom-call(f32[4,8,128]{2,1,0:T(8,128)S(1)} %maximum_bitcast_fusion.own, f32[4,8,128]{2,1,0:T(8,128)S(1)} %collective-permute-done.up, f32[4,8,128]{2,1,0:T(8,128)S(1)} %collective-permute-done.1.down, f32[32,8,128]{2,1,0:T(8,128)S(1)} %get-tuple-element.16.members), custom_call_target="tpu_custom_call" | custom-call | flops 28835840 | bytes 2883584 | tf_op jit(solution)/shard_map/factor/pallas_call | solution.py:212
  87.2 0.2 collective-permute-done.3.mine_up
  87.4 0.6 all-to-all-done.2
  88.0 10.6 %all_to_all.21 = f32[8,16,4,128]{3,2,1,0:T(4,128)S(1)} all-to-all(f32[8,16,4,128]{3,2,1,0:T(4,128)S(1)} %broadcast_in_dim.11), channel_id=1, replica_groups=mesh['slab'=8,'z'=16,'x'=4,'core'=2] {'x','core'}, dimensions={0} | all-to-all | bytes 524288 | tf_op jit(solution)/shard_map/all_to_all | solution.py:164
  98.6 3.4 %force.1 = f32[4,3,128]{2,1,0:T(4,128)S(1)} custom-call(s32[4,8]{1,0:T(4,128)S(1)} %copy-done, s32[4]{0:T(128)S(1)} %copy-done.1, f32[4,8,128]{2,1,0:T(8,128)S(1)} %maximum_bitcast_fusion.own, f32[4,8,128]{2,1,0:T(8,128)S(1)} %collective-permute-done.up, f32[4,8,128]{2,1,0:T(8,128)S(1)} %collective-permute-done.1.down, ...), custom_call_target="tpu_custom_call" | custom-call | flops 14417920 | bytes 2883584 | tf_op jit(solution)/shard_map/force/pallas_call | solution.py:225
  102.0 0.6 copy.7
  (10 shorter events, 0.2 us)
Async XLA Ops:
  0.6 60.9 %copy-start.1 = (s32[4]{0:T(128)S(1)}, s32[4]{0:T(128)}, u32[]{:S(2)}) copy-start(s32[4]{0:T(128)} %counts.3) | copy-start | bytes 52
  0.6 60.9 %copy-start = (s32[4,8]{1,0:T(4,128)S(1)}, s32[4,8]{1,0:T(4,128)}, u32[]{:S(2)}) copy-start(s32[4,8]{1,0:T(4,128)} %partners.3) | copy-start | bytes 388
  3.5 33.2 %all-to-all-start = ((f32[16,4,8,128]{3,2,1,0:T(8,128)}), f32[16,4,8,128]{3,2,1,0:T(8,128)S(1)}, u32[]{:S(2)}, u32[]{:S(2)}) async-start(f32[16,4,8,128]{3,2,1,0:T(8,128)} %broadcast_in_dim.8), calls=%async_computation | async-start | bytes 524288 | tf_op jit(solution)/shard_map/all_to_all | solution.py:164
  22.9 7.0 %collective-permute-start.1 = (f32[4,8,128]{2,1,0:T(8,128)S(1)}, f32[4,8,128]{2,1,0:T(8,128)S(1)}, u32[]{:S(2)}, u32[]{:S(2)}) collective-permute-start(f32[4,8,128]{2,1,0:T(8,128)S(1)} %maximum_bitcast_fusion.own), channel_id=1, source_target_pairs={{128,0},{256,128},{384,256},{512,384},{640,512},{768,640},{896,768... | collective-permute-start | bytes 49160 | tf_op jit(solution)/shard_map/ppermute | solution.py:159
  28.1 6.0 %collective-permute-start = (f32[4,8,128]{2,1,0:T(8,128)S(1)}, f32[4,8,128]{2,1,0:T(8,128)S(1)}, u32[]{:S(2)}, u32[]{:S(2)}) collective-permute-start(f32[4,8,128]{2,1,0:T(8,128)S(1)} %maximum_bitcast_fusion.own), channel_id=1, source_target_pairs={{0,128},{128,256},{256,384},{384,512},{512,640},{640,768},{768,896... | collective-permute-start | bytes 49160 | tf_op jit(solution)/shard_map/ppermute | solution.py:159
  50.4 11.2 %collective-permute-start.2 = (f32[256,8,128]{2,1,0:T(8,128)S(1)}, f32[256,8,128]{2,1,0:T(8,128)S(1)}, u32[]{:S(2)}, u32[]{:S(2)}) collective-permute-start(f32[256,8,128]{2,1,0:T(8,128)S(1)} %bitcast.6), channel_id=1, source_target_pairs={{0,1},{1,0},{2,3},{3,2},{4,5},{5,4},{6,7},{7,6},{8,9},{9,8},{10,11... | collective-permute-start | bytes 3145736 | tf_op jit(solution)/shard_map/ppermute | solution.py:195
  66.8 21.1 %all-to-all-start.2 = ((f32[16,4,128]{2,1,0:T(4,128)}), f32[16,4,128]{2,1,0:T(4,128)S(1)}, u32[]{:S(2)}, u32[]{:S(2)}) async-start(f32[16,4,128]{2,1,0:T(4,128)} %broadcast_in_dim.10), calls=%async_computation.2 | async-start | bytes 65536 | tf_op jit(solution)/shard_map/all_to_all | solution.py:164
  76.5 10.7 %collective-permute-start.4 = (f32[4,128]{1,0:T(4,128)S(1)}, f32[4,128]{1,0:T(4,128)S(1)}, u32[]{:S(2)}, u32[]{:S(2)}) collective-permute-start(f32[4,128]{1,0:T(4,128)S(1)} %get-tuple-element.18.mine), channel_id=1, source_target_pairs={{128,0},{256,128},{384,256},{512,384},{640,512},{768,640},{896,768... | collective-permute-start | bytes 6152 | tf_op jit(solution)/shard_map/ppermute | solution.py:159
  81.6 5.8 %collective-permute-start.3 = (f32[4,128]{1,0:T(4,128)S(1)}, f32[4,128]{1,0:T(4,128)S(1)}, u32[]{:S(2)}, u32[]{:S(2)}) collective-permute-start(f32[4,128]{1,0:T(4,128)S(1)} %get-tuple-element.18.mine), channel_id=1, source_target_pairs={{0,128},{128,256},{256,384},{384,512},{512,640},{640,768},{768,896... | collective-permute-start | bytes 6152 | tf_op jit(solution)/shard_map/ppermute | solution.py:159

commit v4 on v3

v4 whole, which is shorter than its diff:
```python
import jax
import jax.numpy as jnp
from jax import lax
from jax.experimental import pallas as pl
from jax.experimental.pallas import tpu as pltpu
from jax.sharding import Mesh, PartitionSpec as P

weight_norm = 21.0 / (16.0 * 3.141592653589793)
force_norm = 105.0 / (16.0 * 3.141592653589793)
viscosity = 0.25

BINS = 4
LINKS = 8
SLOTS = 128
ROWS = 8
COUNT = 3 + LINKS
CHUNKS = SLOTS // 8
F32 = jnp.float32
VMEM = pl.BlockSpec(memory_space=pltpu.MemorySpace.VMEM)
SMEM = pl.BlockSpec(memory_space=pltpu.MemorySpace.SMEM)
ANY = pl.BlockSpec(memory_space=pl.ANY)


def shape(*dims):
    return jax.ShapeDtypeStruct(dims, F32)


def root(square):
    return square * lax.rsqrt(jnp.maximum(square, 1e-36))


def columns(tall, c, rows):
    cols = tall[c * 8 : c * 8 + 8, :]
    return [jnp.broadcast_to(cols[:, r : r + 1], (8, SLOTS)) for r in rows]


def density_terms(tall, others, acc):
    for c in range(CHUNKS):
        xi, yi, zi, hi = columns(tall, c, (0, 1, 2, 6))
        inv = 0.5 / hi
        total = jnp.zeros((8, SLOTS), F32)
        for row in others:
            dx = xi - row(0)
            dy = yi - row(1)
            dz = zi - row(2)
            s = jnp.maximum(1.0 - root(dx * dx + dy * dy + dz * dz) * inv, 0.0)
            s2 = s * s
            total = total + (s2 * s2) * (5.0 - 4.0 * s) * row(7)
        acc[c * 8 : c * 8 + 8, :] = total * (weight_norm / (hi * hi * hi))
    return jnp.sum(acc[...].T, axis=0, keepdims=True)


def reader(ref, *index):
    return lambda r: ref[(*index, pl.ds(r, 8, stride=0), slice(None))]


def prepare_kernel(counts, particles, own, block):
    lane = lax.broadcasted_iota(jnp.int32, (1, SLOTS), 1)
    for b in range(BINS):
        filled = (lane < counts[b]).astype(F32)
        for r in range(ROWS):
            row = particles[r, b : b + 1, :]
            own[b, r : r + 1, :] = row * filled if r == 7 else row
        tile = own[b]
        for copy in range(block.shape[0]):
            block[copy, b] = tile


def factor_terms(tall, others, store, acc):
    for c in range(CHUNKS):
        xi, yi, zi, hi = columns(tall, c, (0, 1, 2, 6))
        ax = jnp.zeros((8, SLOTS), F32)
        ay, az = ax, ax
        for j, row in enumerate(others):
            dx = xi - row(0)
            dy = yi - row(1)
            dz = zi - row(2)
            inv = 1.0 / (hi + row(6))
            s = jnp.maximum(1.0 - root(dx * dx + dy * dy + dz * dz) * inv, 0.0) * inv
            factor = (s * s * s) * (inv * inv) * row(7)
            store[0, j, c * 8 : c * 8 + 8, :] = factor
            ax = ax + factor * dx
            ay = ay + factor * dy
            az = az + factor * dz
        for d, total in enumerate((ax, ay, az)):
            acc[d, c * 8 : c * 8 + 8, :] = total
    return [jnp.sum(acc[d].T, axis=0, keepdims=True) for d in range(3)]


def near_kernel(own, up, down, part, factors, base, tall, acc, acc3):
    tall[...] = own[0].T
    others = [reader(ref, 0) for ref in (own, up, down)]
    part[0] = density_terms(tall, others, acc)
    for d, total in enumerate(factor_terms(tall, others, factors, acc3)):
        base[0, d : d + 1, :] = total


def partner_density_kernel(partners, counts, own, part, near, far, den_out, inv_out, block, members, tall, acc, sems):
    me = lax.axis_index("core")

    def copies(b, k):
        bin_id = partners[b, k]
        index = (((bin_id >> 3) & 3) * 16 + (bin_id >> 5)) * BINS + (bin_id & 3)
        at = b * LINKS + k
        mine = ((bin_id >> 2) & 1) == me
        return mine, [pltpu.make_async_copy(ref.at[index], members.at[at], sems.at[at]) for ref in (near, far)]

    for b in range(BINS):
        for k in range(LINKS):
            mine, (from_near, from_far) = copies(b, k)
            pl.when(mine)(from_near.start)
            pl.when(jnp.logical_not(mine))(from_far.start)

    def per_bin(b, carry):
        tall[...] = own[b].T
        for k in range(LINKS):
            at = b * LINKS + k
            pltpu.make_async_copy(near.at[0], members.at[at], sems.at[at]).wait()
        far_part = density_terms(tall, [reader(members, b * LINKS + k) for k in range(LINKS)], acc)
        raw = part[b] + far_part
        lane = lax.broadcasted_iota(jnp.int32, (1, SLOTS), 1)
        filled = (lane < counts[b]).astype(F32)
        den_out[pl.ds(b, 1), :] = filled * raw
        inv_out[pl.ds(b, 1), :] = 1.0 / (filled * raw + (1.0 - filled))
        return carry

    lax.fori_loop(0, BINS, per_bin, 0)
    inverse = inv_out[...]
    for copy in range(block.shape[0]):
        block[copy] = inverse


def factor_kernel(own, members, factors, base, tall, acc3):
    tall[...] = own[0].T
    for d, total in enumerate(factor_terms(tall, [reader(members, k) for k in range(LINKS)], factors, acc3)):
        base[0, d : d + 1, :] = total


def force_kernel(
    partners,
    counts,
    own,
    up,
    down,
    members,
    near_factors,
    far_factors,
    near_base,
    far_base,
    mine,
    mine_up,
    mine_down,
    inverse,
    out,
    weights,
    tall,
    acc,
):
    b = pl.program_id(0)
    for j, ref in enumerate((mine, mine_up, mine_down)):
        weights[j : j + 1, :] = ref[pl.ds(b, 1), :]
    for k in range(LINKS):
        bin_id = partners[b, k]
        at = ((bin_id >> 2) & 1) * 256 + (bin_id >> 3) * BINS + (bin_id & 3)
        weights[3 + k : 4 + k, :] = inverse[pl.ds(at, 1), :]
    tall[...] = own[0].T
    others = [(reader(ref, 0), near_factors, j) for j, ref in enumerate((own, up, down))]
    others += [(reader(members, k), far_factors, k) for k in range(LINKS)]
    for c in range(CHUNKS):
        xi, yi, zi, ui, vi, wi = columns(tall, c, range(6))
        ax = jnp.zeros((8, SLOTS), F32)
        ay, az, bx, by, bz = (ax,) * 5
        for j, (row, factors, at) in enumerate(others):
            factor = factors[0, at, c * 8 : c * 8 + 8, :] * weights[pl.ds(j, 8, stride=0), :]
            ax = ax + factor * (xi - row(0))
            ay = ay + factor * (yi - row(1))
            az = az + factor * (zi - row(2))
            bx = bx + factor * (ui - row(3))
            by = by + factor * (vi - row(4))
            bz = bz + factor * (wi - row(5))
        for d, total in enumerate((ax, ay, az, bx, by, bz)):
            acc[d, c * 8 : c * 8 + 8, :] = total
    lane = lax.broadcasted_iota(jnp.int32, (1, SLOTS), 1)
    scale = (lane < counts[b]).astype(F32) * (32.0 * force_norm)
    weight = weights[0:1, :]
    for d in range(3):
        push = jnp.sum(acc[d].T, axis=0, keepdims=True)
        drag = jnp.sum(acc[3 + d].T, axis=0, keepdims=True)
        still = near_base[0, d : d + 1, :] + far_base[0, d : d + 1, :]
        out[d, pl.ds(b, 1), :] = (push + weight * (still - viscosity * drag)) * scale


def both_ways(value):
    count = lax.axis_size("slab")
    up = [(i, (i + 1) % count) for i in range(count)]
    down = [(j, i) for i, j in up]
    return lax.ppermute(value, "slab", up), lax.ppermute(value, "slab", down)


def cost(pairs, ops):
    work = pairs * SLOTS * SLOTS
    return pl.CostEstimate(flops=work * ops, bytes_accessed=work * 4, transcendentals=work)


def limit(mib):
    return pltpu.CompilerParams(vmem_limit_bytes=mib << 20)


def per_device(particles, counts, partners):
    layers, cols = lax.axis_size("z"), lax.axis_size("x")
    own, block = pl.pallas_call(
        prepare_kernel,
        out_shape=(shape(BINS, ROWS, SLOTS), shape(layers, BINS, ROWS, SLOTS)),
        in_specs=[SMEM, VMEM],
        out_specs=(VMEM, VMEM),
        compiler_params=limit(8),
        name="prepare",
    )(counts, particles)
    up, down = both_ways(own)
    column = lax.all_to_all(block, "z", 0, 0, tiled=True)
    tall, acc, acc3 = (pltpu.VMEM(dims, F32) for dims in ((SLOTS, ROWS), (SLOTS, SLOTS), (3, SLOTS, SLOTS)))
    tile = pl.BlockSpec((1, ROWS, SLOTS), lambda b: (b, 0, 0))
    links = pl.BlockSpec((LINKS, ROWS, SLOTS), lambda b: (b, 0, 0))
    near_pairs = pl.BlockSpec((1, 3, SLOTS, SLOTS), lambda b: (b, 0, 0, 0))
    far_pairs = pl.BlockSpec((1, LINKS, SLOTS, SLOTS), lambda b: (b, 0, 0, 0))
    row = pl.BlockSpec((1, 1, SLOTS), lambda b: (b, 0, 0))
    vector = pl.BlockSpec((1, 3, SLOTS), lambda b: (b, 0, 0))
    part, near_factors, near_base = pl.pallas_call(
        near_kernel,
        grid=(BINS,),
        out_shape=(shape(BINS, 1, SLOTS), shape(BINS, 3, SLOTS, SLOTS), shape(BINS, 3, SLOTS)),
        in_specs=[tile] * 3,
        out_specs=(row, near_pairs, vector),
        scratch_shapes=[tall, acc, acc3],
        cost_estimate=cost(3 * BINS, 60),
        compiler_params=limit(8),
        name="near",
    )(own, up, down)
    column, part, near_factors, near_base = lax.optimization_barrier((column, part, near_factors, near_base))
    near = lax.all_to_all(jnp.broadcast_to(column[None], (cols,) + column.shape), "x", 0, 0, tiled=True)
    near = near.reshape(-1, ROWS, SLOTS)
    far = lax.ppermute(near, "core", [(0, 1), (1, 0)])
    density, mine, block, members = pl.pallas_call(
        partner_density_kernel,
        out_shape=(
            shape(BINS, SLOTS),
            shape(BINS, SLOTS),
            shape(layers * cols, BINS, SLOTS),
            shape(BINS * LINKS, ROWS, SLOTS),
        ),
        in_specs=[SMEM, SMEM, VMEM, VMEM, ANY, ANY],
        out_specs=(VMEM,) * 4,
        scratch_shapes=[tall, acc, pltpu.SemaphoreType.DMA((BINS * LINKS,))],
        cost_estimate=cost(LINKS * BINS, 20),
        compiler_params=limit(8),
        name="partner_density",
    )(partners, counts, own, part, near, far)
    mine_up, mine_down = both_ways(mine)
    inverse = lax.all_to_all(block, ("z", "x"), 0, 0, tiled=True)
    far_factors, far_base = pl.pallas_call(
        factor_kernel,
        grid=(BINS,),
        out_shape=(shape(BINS, LINKS, SLOTS, SLOTS), shape(BINS, 3, SLOTS)),
        in_specs=[tile, links],
        out_specs=(far_pairs, vector),
        scratch_shapes=[tall, acc3],
        cost_estimate=cost(LINKS * BINS, 40),
        compiler_params=limit(8),
        name="factor",
    )(own, members)
    inverse, far_base, mine_up, mine_down = lax.optimization_barrier((inverse, far_base, mine_up, mine_down))
    inverse = lax.all_gather(inverse.reshape(-1, SLOTS), "core", axis=0, tiled=True)
    acceleration = pl.pallas_call(
        force_kernel,
        grid=(BINS,),
        out_shape=shape(3, BINS, SLOTS),
        in_specs=[SMEM, SMEM, tile, tile, tile, links, near_pairs, far_pairs, vector, vector] + [VMEM] * 4,
        out_specs=pl.BlockSpec((3, BINS, SLOTS), lambda b: (0, 0, 0)),
        scratch_shapes=[pltpu.VMEM((16, SLOTS), F32), tall, pltpu.VMEM((6, SLOTS, SLOTS), F32)],
        cost_estimate=cost(COUNT * BINS, 20),
        compiler_params=limit(8),
        name="force",
    )(
        partners,
        counts,
        own,
        up,
        down,
        members,
        near_factors,
        far_factors,
        near_base,
        far_base,
        mine,
        mine_up,
        mine_down,
        inverse,
    )
    return density, acceleration


def solution(mesh):
    grid = Mesh(mesh.devices.reshape(mesh.shape["slab"], 16, 4, 2), ("slab", "z", "x", "core"))
    axes = ("slab", "z", "x", "core")
    return jax.shard_map(
        per_device,
        mesh=grid,
        in_specs=(P(None, axes, None), P(axes), P(axes, None)),
        out_specs=(P(axes, None), P(None, axes, None)),
        check_vma=False,
    )
```

time: 103 us -> 103 us (level)
  blocking collectives: 24.2 us -> 18.6 us
  waiting for transfers between devices: 8.18 us -> 12.7 us
  local copies, waits for them, and re-layouts: 3.52 us -> 1.49 us
  Pallas kernels: 13.3 us -> 15.3 us
  starting transfers between devices: 52 us -> 53.6 us
    all_to_all x2 -> x1, blocking collectives: 24.2 us -> 13.6 us  [per_device(): lax.all_to_all(jnp.broadcast_to(column[None], (cols,) + column.shape), 'x...]
    all_gather x0 -> x1, blocking collectives: none -> 5.03 us  [per_device(): lax.all_gather(inverse.reshape(-1, SLOTS), 'core', axis=0, tiled=True)]
    all_to_all x2, waiting for transfers between devices: 1.68 us -> 5.41 us  [the longest x1 5.14 us: per_device(): inverse = lax.all_to_all(block, ('z', 'x'), 0, 0, tiled=True)]
    all_to_all x2, starting transfers between devices: 29.1 us -> 31.6 us  [the longest x1 19.5 us: per_device(): column = lax.all_to_all(block, 'z', 0, 0, tiled=True)]
    pallas_call x3 -> x4, Pallas kernels: 8.64 us -> 10.6 us  [the longest x1 3.97 us: per_device(): pl.pallas_call(force_kernel, grid=(BINS,), out_shape=shape(3, BINS, SLOTS...]
    slice x2 -> x0, local copies, waits for them, and re-layouts: 1.41 us -> none  [the longest x1 0.71 us: per_device(): particles[:7]]
    broadcast_in_dim x4 -> x1, local copies, waits for them, and re-layouts: 1.5 us -> 0.12 us  [per_device(): jnp.broadcast_to(column[None], (cols,) + column.shape)]
where the time goes in v4:
time: 103 us; the launch traced here: 102 us
  starting transfers between devices  53.6 us (52%)
  blocking collectives  18.6 us (18%)
  Pallas kernels  15.3 us (15%)
  waiting for transfers between devices  12.7 us (12%)
  local copies, waits for them, and re-layouts  1.49 us (1%)
    all_to_all x1, starting transfers between devices, per_device(): column = lax.all_to_all(block, 'z', 0, 0, tiled=True)  19.5 us
    all_to_all x1, blocking collectives, per_device(): lax.all_to_all(jnp.broadcast_to(column[None], (cols,) + column.shape), 'x...  13.6 us
    ppermute x4, starting transfers between devices, both_ways(): return (lax.ppermute(value, 'slab', up), lax.ppermute(value, 'slab', down))  13.2 us
    all_to_all x1, starting transfers between devices, per_device(): inverse = lax.all_to_all(block, ('z', 'x'), 0, 0, tiled=True)  12 us
    ppermute x1, starting transfers between devices, per_device(): far = lax.ppermute(near, 'core', [(0, 1), (1, 0)])  8.89 us
    all_to_all x1, waiting for transfers between devices, per_device(): inverse = lax.all_to_all(block, ('z', 'x'), 0, 0, tiled=True)  5.14 us
    all_gather x1, blocking collectives, per_device(): lax.all_gather(inverse.reshape(-1, SLOTS), 'core', axis=0, tiled=True)  5.03 us
    ppermute x4, waiting for transfers between devices, both_ways(): return (lax.ppermute(value, 'slab', up), lax.ppermute(value, 'slab', down))  5 us
  transfers between devices with their start and end apart: 7, of which 5 were waited for; matrix products, arithmetic and copies ran while one was open for 0% of the time, Pallas kernels for 5%

profile of v4, /device:TPU:1, one launch (start us, length us, event | category | flops | bytes accessed | tf_op | source)
XLA Modules:
  0.0 102.4 jit_solution(11585349460591179179)
XLA Ops:
  0.6 0.7 copy-done
  1.3 0.7 copy-done.2
  2.0 1.3 %prepare.1 = (f32[4,8,128]{2,1,0:T(8,128)S(1)}, f32[16,4,8,128]{3,2,1,0:T(8,128)}) custom-call(s32[4]{0:T(128)S(1)} %copy-done.2, f32[8,4,128]{2,1,0:T(4,128)S(1)} %copy-done), custom_call_target="tpu_custom_call" | custom-call | tf_op jit(solution)/shard_map/prepare/pallas_call | solution.py:211
  3.3 19.5 %all-to-all-start = ((f32[16,4,8,128]{3,2,1,0:T(8,128)}), f32[16,4,8,128]{3,2,1,0:T(8,128)S(1)}, u32[]{:S(2)}, u32[]{:S(2)}) async-start(f32[16,4,8,128]{3,2,1,0:T(8,128)} %get-tuple-element.22), calls=%async_computation | async-start | bytes 524288 | tf_op jit(solution)/shard_map/all_to_all | solution.py:220
  22.8 5.1 %collective-permute-start.1 = (f32[4,8,128]{2,1,0:T(8,128)S(1)}, f32[4,8,128]{2,1,0:T(8,128)S(1)}, u32[]{:S(2)}, u32[]{:S(2)}) collective-permute-start(f32[4,8,128]{2,1,0:T(8,128)S(1)} %get-tuple-element.21.own), channel_id=1, source_target_pairs={{128,0},{256,128},{384,256},{512,384},{640,512},{768,640},{896,768... | collective-permute-start | bytes 49160 | tf_op jit(solution)/shard_map/ppermute | solution.py:197
  27.9 1.9 %collective-permute-start = (f32[4,8,128]{2,1,0:T(8,128)S(1)}, f32[4,8,128]{2,1,0:T(8,128)S(1)}, u32[]{:S(2)}, u32[]{:S(2)}) collective-permute-start(f32[4,8,128]{2,1,0:T(8,128)S(1)} %get-tuple-element.21.own), channel_id=1, source_target_pairs={{0,128},{128,256},{256,384},{384,512},{512,640},{640,768},{768,896... | collective-permute-start | bytes 49160 | tf_op jit(solution)/shard_map/ppermute | solution.py:197
  29.9 0.0 collective-permute-done.1.down
  29.9 4.0 %collective-permute-done.up = f32[4,8,128]{2,1,0:T(8,128)S(1)} collective-permute-done((f32[4,8,128]{2,1,0:T(8,128)S(1)}, f32[4,8,128]{2,1,0:T(8,128)S(1)}, u32[]{:S(2)}, u32[]{:S(2)}) %collective-permute-start) | collective-permute-done | bytes 16416 | tf_op jit(solution)/shard_map/ppermute | solution.py:197
  33.9 2.4 %near.1 = (f32[4,1,128]{2,1,0:T(1,128)S(1)}, f32[4,3,128,128]{3,2,1,0:T(8,128)S(1)}, f32[4,3,128]{2,1,0:T(4,128)S(1)}) custom-call(f32[4,8,128]{2,1,0:T(8,128)S(1)} %get-tuple-element.21.own, f32[4,8,128]{2,1,0:T(8,128)S(1)} %collective-permute-done.up, f32[4,8,128]{2,1,0:T(8,128)S(1)} %collective-permute-done.1.down), custom_call_target="tpu_custom_call" | custom-call | flops 11796480 | bytes 786432 | tf_op jit(solution)/shard_map/near/pallas_call | solution.py:228
  36.3 0.3 all-to-all-done
  36.6 0.1 broadcast_in_dim.2
  36.7 13.6 %all_to_all.15 = f32[4,16,4,8,128]{4,3,2,1,0:T(8,128)S(1)} all-to-all(f32[4,16,4,8,128]{4,3,2,1,0:T(8,128)S(1)} %broadcast_in_dim.2), channel_id=1, replica_groups=mesh['slab'=8,'z'=16,'x'=4,'core'=2] {'x'}, dimensions={0} | all-to-all | bytes 2097152 | tf_op jit(solution)/shard_map/all_to_all | solution.py:240
  50.3 8.9 %collective-permute-start.2 = (f32[256,8,128]{2,1,0:T(8,128)S(1)}, f32[256,8,128]{2,1,0:T(8,128)S(1)}, u32[]{:S(2)}, u32[]{:S(2)}) collective-permute-start(f32[256,8,128]{2,1,0:T(8,128)S(1)} %bitcast.2), channel_id=1, source_target_pairs={{0,1},{1,0},{2,3},{3,2},{4,5},{5,4},{6,7},{7,6},{8,9},{9,8},{10,11... | collective-permute-start | bytes 3145736 | tf_op jit(solution)/shard_map/ppermute | solution.py:242
  59.2 2.3 %collective-permute-done.2.far = f32[256,8,128]{2,1,0:T(8,128)S(1)} collective-permute-done((f32[256,8,128]{2,1,0:T(8,128)S(1)}, f32[256,8,128]{2,1,0:T(8,128)S(1)}, u32[]{:S(2)}, u32[]{:S(2)}) %collective-permute-start.2) | collective-permute-done | bytes 1048608 | tf_op jit(solution)/shard_map/ppermute | solution.py:242
  61.4 4.7 %partner_density.1 = (f32[4,128]{1,0:T(4,128)}, f32[4,128]{1,0:T(4,128)S(1)}, f32[64,4,128]{2,1,0:T(4,128)}, f32[32,8,128]{2,1,0:T(8,128)S(1)}) custom-call(s32[4,8]{1,0:T(4,128)S(1)} %copy-done.1, s32[4]{0:T(128)S(1)} %copy-done.3, f32[4,8,128]{2,1,0:T(8,128)S(1)} %get-tuple-element.21.own, f32[4,1,128]{2,1,0:T(1,128)S(1)} %get-tuple-element.26.part, ...), custom_call_target="tpu_custom_call" | custom-call | flops 10485760 | bytes 2097152 | tf_op jit(solution)/shard_map/partner_density/pallas_call | solution.py:243
  66.2 12.0 %all-to-all-start.2 = ((f32[64,4,128]{2,1,0:T(4,128)}), f32[64,4,128]{2,1,0:T(4,128)S(1)}, u32[]{:S(2)}, u32[]{:S(2)}) async-start(f32[64,4,128]{2,1,0:T(4,128)} %get-tuple-element.33), calls=%async_computation.2 | async-start | bytes 262144 | tf_op jit(solution)/shard_map/all_to_all | solution.py:259
  78.2 4.2 %collective-permute-start.4 = (f32[4,128]{1,0:T(4,128)S(1)}, f32[4,128]{1,0:T(4,128)S(1)}, u32[]{:S(2)}, u32[]{:S(2)}) collective-permute-start(f32[4,128]{1,0:T(4,128)S(1)} %get-tuple-element.35.mine), channel_id=1, source_target_pairs={{128,0},{256,128},{384,256},{512,384},{640,512},{768,640},{896,768... | collective-permute-start | bytes 6152 | tf_op jit(solution)/shard_map/ppermute | solution.py:197
  82.5 1.9 %collective-permute-start.3 = (f32[4,128]{1,0:T(4,128)S(1)}, f32[4,128]{1,0:T(4,128)S(1)}, u32[]{:S(2)}, u32[]{:S(2)}) collective-permute-start(f32[4,128]{1,0:T(4,128)S(1)} %get-tuple-element.35.mine), channel_id=1, source_target_pairs={{0,128},{128,256},{256,384},{384,512},{512,640},{640,768},{768,896... | collective-permute-start | bytes 6152 | tf_op jit(solution)/shard_map/ppermute | solution.py:197
  84.4 2.9 %factor.1 = (f32[4,8,128,128]{3,2,1,0:T(8,128)S(1)}, f32[4,3,128]{2,1,0:T(4,128)S(1)}) custom-call(f32[4,8,128]{2,1,0:T(8,128)S(1)} %get-tuple-element.21.own, f32[32,8,128]{2,1,0:T(8,128)S(1)} %get-tuple-element.29.members), custom_call_target="tpu_custom_call" | custom-call | flops 20971520 | bytes 2097152 | tf_op jit(solution)/shard_map/factor/pallas_call | solution.py:260
  87.3 0.0 collective-permute-done.4.mine_down
  87.4 0.9 collective-permute-done.3.mine_up
  88.3 5.1 %all-to-all-done.2 = f32[64,4,128]{2,1,0:T(4,128)S(1)} async-done(((f32[64,4,128]{2,1,0:T(4,128)}), f32[64,4,128]{2,1,0:T(4,128)S(1)}, u32[]{:S(2)}, u32[]{:S(2)}) %all-to-all-start.2) | async-done | bytes 131104 | tf_op jit(solution)/shard_map/all_to_all | solution.py:259
  93.4 5.0 %all_gather.3.inverse = f32[512,128]{1,0:T(8,128)S(1)} all-gather(f32[256,128]{1,0:T(8,128)S(1)} %bitcast.4), channel_id=1, replica_groups=mesh['slab'=8,'z'=16,'x'=4,'core'=2] {'core'}, dimensions={0}, use_global_device_ids=true | all-gather | bytes 393216 | tf_op jit(solution)/shard_map/all_gather | solution.py:272
  98.5 4.0 %force.1 = f32[3,4,128]{2,1,0:T(4,128)} custom-call(s32[4,8]{1,0:T(4,128)S(1)} %copy-done.1, s32[4]{0:T(128)S(1)} %copy-done.3, f32[4,8,128]{2,1,0:T(8,128)S(1)} %get-tuple-element.21.own, f32[4,8,128]{2,1,0:T(8,128)S(1)} %collective-permute-done.up, f32[4,8,128]{2,1,0:T(8,128)S(1)} %collective-permute-done.1.down, ...), custom_call_target="tpu_custom_call" | custom-call | flops 14417920 | bytes 2883584 | tf_op jit(solution)/shard_map/force/pallas_call | solution.py:273
  (6 shorter events, 0.0 us)
Async XLA Ops:
  0.6 0.7 copy-start
  1.3 0.7 copy-start.2
  3.3 58.2 %copy-start.1 = (s32[4,8]{1,0:T(4,128)S(1)}, s32[4,8]{1,0:T(4,128)}, u32[]{:S(2)}) copy-start(s32[4,8]{1,0:T(4,128)} %partners.3) | copy-start | bytes 388
  3.3 58.2 %copy-start.3 = (s32[4]{0:T(128)S(1)}, s32[4]{0:T(128)}, u32[]{:S(2)}) copy-start(s32[4]{0:T(128)} %counts.5) | copy-start | bytes 52
  3.3 33.3 %all-to-all-start = ((f32[16,4,8,128]{3,2,1,0:T(8,128)}), f32[16,4,8,128]{3,2,1,0:T(8,128)S(1)}, u32[]{:S(2)}, u32[]{:S(2)}) async-start(f32[16,4,8,128]{3,2,1,0:T(8,128)} %get-tuple-element.22), calls=%async_computation | async-start | bytes 524288 | tf_op jit(solution)/shard_map/all_to_all | solution.py:220
  22.8 7.0 %collective-permute-start.1 = (f32[4,8,128]{2,1,0:T(8,128)S(1)}, f32[4,8,128]{2,1,0:T(8,128)S(1)}, u32[]{:S(2)}, u32[]{:S(2)}) collective-permute-start(f32[4,8,128]{2,1,0:T(8,128)S(1)} %get-tuple-element.21.own), channel_id=1, source_target_pairs={{128,0},{256,128},{384,256},{512,384},{640,512},{768,640},{896,768... | collective-permute-start | bytes 49160 | tf_op jit(solution)/shard_map/ppermute | solution.py:197
  27.9 6.0 %collective-permute-start = (f32[4,8,128]{2,1,0:T(8,128)S(1)}, f32[4,8,128]{2,1,0:T(8,128)S(1)}, u32[]{:S(2)}, u32[]{:S(2)}) collective-permute-start(f32[4,8,128]{2,1,0:T(8,128)S(1)} %get-tuple-element.21.own), channel_id=1, source_target_pairs={{0,128},{128,256},{256,384},{384,512},{512,640},{640,768},{768,896... | collective-permute-start | bytes 49160 | tf_op jit(solution)/shard_map/ppermute | solution.py:197
  50.3 11.2 %collective-permute-start.2 = (f32[256,8,128]{2,1,0:T(8,128)S(1)}, f32[256,8,128]{2,1,0:T(8,128)S(1)}, u32[]{:S(2)}, u32[]{:S(2)}) collective-permute-start(f32[256,8,128]{2,1,0:T(8,128)S(1)} %bitcast.2), channel_id=1, source_target_pairs={{0,1},{1,0},{2,3},{3,2},{4,5},{5,4},{6,7},{7,6},{8,9},{9,8},{10,11... | collective-permute-start | bytes 3145736 | tf_op jit(solution)/shard_map/ppermute | solution.py:242
  66.2 27.2 %all-to-all-start.2 = ((f32[64,4,128]{2,1,0:T(4,128)}), f32[64,4,128]{2,1,0:T(4,128)S(1)}, u32[]{:S(2)}, u32[]{:S(2)}) async-start(f32[64,4,128]{2,1,0:T(4,128)} %get-tuple-element.33), calls=%async_computation.2 | async-start | bytes 262144 | tf_op jit(solution)/shard_map/all_to_all | solution.py:259
  78.2 9.1 %collective-permute-start.4 = (f32[4,128]{1,0:T(4,128)S(1)}, f32[4,128]{1,0:T(4,128)S(1)}, u32[]{:S(2)}, u32[]{:S(2)}) collective-permute-start(f32[4,128]{1,0:T(4,128)S(1)} %get-tuple-element.35.mine), channel_id=1, source_target_pairs={{128,0},{256,128},{384,256},{512,384},{640,512},{768,640},{896,768... | collective-permute-start | bytes 6152 | tf_op jit(solution)/shard_map/ppermute | solution.py:197
  82.5 5.8 %collective-permute-start.3 = (f32[4,128]{1,0:T(4,128)S(1)}, f32[4,128]{1,0:T(4,128)S(1)}, u32[]{:S(2)}, u32[]{:S(2)}) collective-permute-start(f32[4,128]{1,0:T(4,128)S(1)} %get-tuple-element.35.mine), channel_id=1, source_target_pairs={{0,128},{128,256},{256,384},{384,512},{512,640},{640,768},{768,896... | collective-permute-start | bytes 6152 | tf_op jit(solution)/shard_map/ppermute | solution.py:197

commit v5 on v4

v5 whole, which is shorter than its diff:
```python
import jax
import jax.numpy as jnp
from jax import lax
from jax.experimental import pallas as pl
from jax.experimental.pallas import tpu as pltpu
from jax.sharding import Mesh, PartitionSpec as P

weight_norm = 21.0 / (16.0 * 3.141592653589793)
force_norm = 105.0 / (16.0 * 3.141592653589793)
viscosity = 0.25

BINS = 4
LINKS = 8
SLOTS = 128
ROWS = 8
COUNT = 3 + LINKS
CHUNKS = SLOTS // 8
F32 = jnp.float32
VMEM = pl.BlockSpec(memory_space=pltpu.MemorySpace.VMEM)
SMEM = pl.BlockSpec(memory_space=pltpu.MemorySpace.SMEM)
HBM = pl.BlockSpec(memory_space=pltpu.MemorySpace.HBM)


def shape(*dims):
    return jax.ShapeDtypeStruct(dims, F32)


def root(square):
    return square * lax.rsqrt(jnp.maximum(square, 1e-36))


def columns(tall, c, rows):
    cols = tall[c * 8 : c * 8 + 8, :]
    return [jnp.broadcast_to(cols[:, r : r + 1], (8, SLOTS)) for r in rows]


def density_terms(tall, others, acc):
    for c in range(CHUNKS):
        xi, yi, zi, hi = columns(tall, c, (0, 1, 2, 6))
        inv = 0.5 / hi
        total = jnp.zeros((8, SLOTS), F32)
        for row in others:
            dx = xi - row(0)
            dy = yi - row(1)
            dz = zi - row(2)
            s = jnp.maximum(1.0 - root(dx * dx + dy * dy + dz * dz) * inv, 0.0)
            s2 = s * s
            total = total + (s2 * s2) * (5.0 - 4.0 * s) * row(7)
        acc[c * 8 : c * 8 + 8, :] = total * (weight_norm / (hi * hi * hi))
    return jnp.sum(acc[...].T, axis=0, keepdims=True)


def reader(ref, *index):
    return lambda r: ref[(*index, pl.ds(r, 8, stride=0), slice(None))]


def prepare_kernel(counts_in, particles_in, own, block, counts, particles, sems):
    fetches = (
        pltpu.make_async_copy(counts_in, counts, sems.at[0]),
        pltpu.make_async_copy(particles_in, particles, sems.at[1]),
    )
    for fetch in fetches:
        fetch.start()
    for fetch in fetches:
        fetch.wait()
    lane = lax.broadcasted_iota(jnp.int32, (1, SLOTS), 1)
    for b in range(BINS):
        filled = (lane < counts[b]).astype(F32)
        for r in range(ROWS):
            row = particles[r, b : b + 1, :]
            own[b, r : r + 1, :] = row * filled if r == 7 else row
        tile = own[b]
        for copy in range(block.shape[0]):
            block[copy, b] = tile


def factor_terms(b, tall, others, store, acc):
    for c in range(CHUNKS):
        xi, yi, zi, hi = columns(tall, c, (0, 1, 2, 6))
        ax = jnp.zeros((8, SLOTS), F32)
        ay, az = ax, ax
        for j, row in enumerate(others):
            dx = xi - row(0)
            dy = yi - row(1)
            dz = zi - row(2)
            inv = 1.0 / (hi + row(6))
            s = jnp.maximum(1.0 - root(dx * dx + dy * dy + dz * dz) * inv, 0.0) * inv
            factor = (s * s * s) * (inv * inv) * row(7)
            store[b, j, c * 8 : c * 8 + 8, :] = factor
            ax = ax + factor * dx
            ay = ay + factor * dy
            az = az + factor * dz
        for d, total in enumerate((ax, ay, az)):
            acc[d, c * 8 : c * 8 + 8, :] = total
    return [jnp.sum(acc[d].T, axis=0, keepdims=True) for d in range(3)]


def near_kernel(own, up, down, part, factors, base, tall, acc, acc3):
    def per_bin(b, carry):
        tall[...] = own[b].T
        others = [reader(ref, b) for ref in (own, up, down)]
        part[pl.ds(b, 1), :] = density_terms(tall, others, acc)
        for d, total in enumerate(factor_terms(b, tall, others, factors, acc3)):
            base[b, d : d + 1, :] = total
        return carry

    lax.fori_loop(0, BINS, per_bin, 0)


def partner_density_kernel(partners, counts, own, part, near, far, den_out, inv_out, block, members, tall, acc):
    me = lax.axis_index("core")

    def per_bin(b, carry):
        for k in range(LINKS):
            bin_id = partners[b, k]
            index = (((bin_id >> 3) & 3) * 16 + (bin_id >> 5)) * BINS + (bin_id & 3)
            mine = ((bin_id >> 2) & 1) == me
            members[b * LINKS + k] = jnp.where(mine, near[index], far[index])
        tall[...] = own[b].T
        far_part = density_terms(tall, [reader(members, b * LINKS + k) for k in range(LINKS)], acc)
        raw = part[pl.ds(b, 1), :] + far_part
        lane = lax.broadcasted_iota(jnp.int32, (1, SLOTS), 1)
        filled = (lane < counts[b]).astype(F32)
        den_out[pl.ds(b, 1), :] = filled * raw
        inv_out[pl.ds(b, 1), :] = 1.0 / (filled * raw + (1.0 - filled))
        return carry

    lax.fori_loop(0, BINS, per_bin, 0)
    inverse = inv_out[...]
    for copy in range(block.shape[0]):
        block[copy] = inverse


def factor_kernel(own, members, factors, base, tall, acc3):
    def per_bin(b, carry):
        tall[...] = own[b].T
        others = [reader(members, b * LINKS + k) for k in range(LINKS)]
        for d, total in enumerate(factor_terms(b, tall, others, factors, acc3)):
            base[b, d : d + 1, :] = total
        return carry

    lax.fori_loop(0, BINS, per_bin, 0)


def force_kernel(
    partners,
    counts,
    own,
    up,
    down,
    members,
    near_factors,
    far_factors,
    near_base,
    far_base,
    mine,
    mine_up,
    mine_down,
    inverse,
    out,
    weights,
    tall,
    acc,
):
    def per_bin(b, carry):
        for j, ref in enumerate((mine, mine_up, mine_down)):
            weights[j : j + 1, :] = ref[pl.ds(b, 1), :]
        for k in range(LINKS):
            bin_id = partners[b, k]
            at = ((bin_id >> 2) & 1) * 256 + (bin_id >> 3) * BINS + (bin_id & 3)
            weights[3 + k : 4 + k, :] = inverse[pl.ds(at, 1), :]
        tall[...] = own[b].T
        others = [(reader(ref, b), near_factors, j) for j, ref in enumerate((own, up, down))]
        others += [(reader(members, b * LINKS + k), far_factors, k) for k in range(LINKS)]
        for c in range(CHUNKS):
            xi, yi, zi, ui, vi, wi = columns(tall, c, range(6))
            ax = jnp.zeros((8, SLOTS), F32)
            ay, az, bx, by, bz = (ax,) * 5
            for j, (row, factors, at) in enumerate(others):
                factor = factors[b, at, c * 8 : c * 8 + 8, :] * weights[pl.ds(j, 8, stride=0), :]
                ax = ax + factor * (xi - row(0))
                ay = ay + factor * (yi - row(1))
                az = az + factor * (zi - row(2))
                bx = bx + factor * (ui - row(3))
                by = by + factor * (vi - row(4))
                bz = bz + factor * (wi - row(5))
            for d, total in enumerate((ax, ay, az, bx, by, bz)):
                acc[d, c * 8 : c * 8 + 8, :] = total
        lane = lax.broadcasted_iota(jnp.int32, (1, SLOTS), 1)
        scale = (lane < counts[b]).astype(F32) * (32.0 * force_norm)
        weight = weights[0:1, :]
        for d in range(3):
            push = jnp.sum(acc[d].T, axis=0, keepdims=True)
            drag = jnp.sum(acc[3 + d].T, axis=0, keepdims=True)
            still = near_base[b, d : d + 1, :] + far_base[b, d : d + 1, :]
            out[d, pl.ds(b, 1), :] = (push + weight * (still - viscosity * drag)) * scale
        return carry

    lax.fori_loop(0, BINS, per_bin, 0)


def both_ways(value):
    count = lax.axis_size("slab")
    up = [(i, (i + 1) % count) for i in range(count)]
    down = [(j, i) for i, j in up]
    return lax.ppermute(value, "slab", up), lax.ppermute(value, "slab", down)


def cost(pairs, ops):
    work = pairs * SLOTS * SLOTS
    return pl.CostEstimate(flops=work * ops, bytes_accessed=work * 4, transcendentals=work)


def limit(mib):
    return pltpu.CompilerParams(vmem_limit_bytes=mib << 20)


def per_device(particles, counts, partners):
    layers, cols = lax.axis_size("z"), lax.axis_size("x")
    own, block = pl.pallas_call(
        prepare_kernel,
        out_shape=(shape(BINS, ROWS, SLOTS), shape(layers, BINS, ROWS, SLOTS)),
        in_specs=[HBM, HBM],
        out_specs=(VMEM, VMEM),
        scratch_shapes=[
            pltpu.SMEM((BINS,), jnp.int32),
            pltpu.VMEM((ROWS, BINS, SLOTS), F32),
            pltpu.SemaphoreType.DMA((2,)),
        ],
        compiler_params=limit(60),
        name="prepare",
    )(counts, particles)
    up, down = both_ways(own)
    column = lax.all_to_all(block, "z", 0, 0, tiled=True)
    tall, acc, acc3 = (pltpu.VMEM(dims, F32) for dims in ((SLOTS, ROWS), (SLOTS, SLOTS), (3, SLOTS, SLOTS)))
    part, near_factors, near_base = pl.pallas_call(
        near_kernel,
        out_shape=(shape(BINS, SLOTS), shape(BINS, 3, SLOTS, SLOTS), shape(BINS, 3, SLOTS)),
        in_specs=[VMEM] * 3,
        out_specs=(VMEM,) * 3,
        scratch_shapes=[tall, acc, acc3],
        cost_estimate=cost(3 * BINS, 60),
        compiler_params=limit(8),
        name="near",
    )(own, up, down)
    column, part, near_factors, near_base = lax.optimization_barrier((column, part, near_factors, near_base))
    near = lax.all_to_all(jnp.broadcast_to(column[None], (cols,) + column.shape), "x", 0, 0, tiled=True)
    near = near.reshape(-1, ROWS, SLOTS)
    far = lax.ppermute(near, "core", [(0, 1), (1, 0)])
    density, mine, block, members = pl.pallas_call(
        partner_density_kernel,
        out_shape=(
            shape(BINS, SLOTS),
            shape(BINS, SLOTS),
            shape(layers * cols, BINS, SLOTS),
            shape(BINS * LINKS, ROWS, SLOTS),
        ),
        in_specs=[SMEM, SMEM] + [VMEM] * 4,
        out_specs=(VMEM,) * 4,
        scratch_shapes=[tall, acc],
        cost_estimate=cost(LINKS * BINS, 20),
        compiler_params=limit(8),
        name="partner_density",
    )(partners, counts, own, part, near, far)
    mine_up, mine_down = both_ways(mine)
    inverse = lax.all_to_all(block, ("z", "x"), 0, 0, tiled=True)
    far_factors, far_base = pl.pallas_call(
        factor_kernel,
        out_shape=(shape(BINS, LINKS, SLOTS, SLOTS), shape(BINS, 3, SLOTS)),
        in_specs=[VMEM] * 2,
        out_specs=(VMEM,) * 2,
        scratch_shapes=[tall, acc3],
        cost_estimate=cost(LINKS * BINS, 40),
        compiler_params=limit(8),
        name="factor",
    )(own, members)
    inverse, far_base, mine_up, mine_down = lax.optimization_barrier((inverse, far_base, mine_up, mine_down))
    inverse = lax.all_gather(inverse.reshape(-1, SLOTS), "core", axis=0, tiled=True)
    acceleration = pl.pallas_call(
        force_kernel,
        out_shape=shape(3, BINS, SLOTS),
        in_specs=[SMEM, SMEM] + [VMEM] * 12,
        out_specs=VMEM,
        scratch_shapes=[pltpu.VMEM((16, SLOTS), F32), tall, pltpu.VMEM((6, SLOTS, SLOTS), F32)],
        cost_estimate=cost(COUNT * BINS, 20),
        compiler_params=limit(8),
        name="force",
    )(
        partners,
        counts,
        own,
        up,
        down,
        members,
        near_factors,
        far_factors,
        near_base,
        far_base,
        mine,
        mine_up,
        mine_down,
        inverse,
    )
    return density, acceleration


def solution(mesh):
    grid = Mesh(mesh.devices.reshape(mesh.shape["slab"], 16, 4, 2), ("slab", "z", "x", "core"))
    axes = ("slab", "z", "x", "core")
    return jax.shard_map(
        per_device,
        mesh=grid,
        in_specs=(P(None, axes, None), P(axes), P(axes, None)),
        out_specs=(P(axes, None), P(None, axes, None)),
        check_vma=False,
    )
```

time: 103 us -> 102 us (level)
  transfers between devices with their start and end apart: 7 -> 7, of which waited for: 5 -> 4; matrix products, arithmetic and copies ran while one was open for 0% -> 0% of each run, Pallas kernels for 5% -> 5%
where the time goes in v5:
time: 102 us; the launch traced here: 101 us
  starting transfers between devices  53 us (52%)
  blocking collectives  18.6 us (18%)
  Pallas kernels  14.8 us (15%)
  waiting for transfers between devices  13.4 us (13%)
    all_to_all x1, starting transfers between devices, per_device(): column = lax.all_to_all(block, 'z', 0, 0, tiled=True)  19.5 us
    all_to_all x1, blocking collectives, per_device(): lax.all_to_all(jnp.broadcast_to(column[None], (cols,) + column.shape), 'x...  13.6 us
    all_to_all x1, starting transfers between devices, per_device(): inverse = lax.all_to_all(block, ('z', 'x'), 0, 0, tiled=True)  12.9 us
    ppermute x4, starting transfers between devices, both_ways(): return (lax.ppermute(value, 'slab', up), lax.ppermute(value, 'slab', down))  12.3 us
    ppermute x1, starting transfers between devices, per_device(): far = lax.ppermute(near, 'core', [(0, 1), (1, 0)])  8.22 us
    all_to_all x1, waiting for transfers between devices, per_device(): inverse = lax.all_to_all(block, ('z', 'x'), 0, 0, tiled=True)  6.07 us
    ppermute x4, waiting for transfers between devices, both_ways(): return (lax.ppermute(value, 'slab', up), lax.ppermute(value, 'slab', down))  5.07 us
    all_gather x1, blocking collectives, per_device(): lax.all_gather(inverse.reshape(-1, SLOTS), 'core', axis=0, tiled=True)  5.02 us
  transfers between devices with their start and end apart: 7, of which 4 were waited for; matrix products, arithmetic and copies ran while one was open for 0% of the time, Pallas kernels for 5%

profile of v5, /device:TPU:1, one launch (start us, length us, event | category | flops | bytes accessed | tf_op | source)
XLA Modules:
  0.0 101.4 jit_solution(3995204549197404976)
XLA Ops:
  0.6 1.5 %prepare.1 = (f32[4,8,128]{2,1,0:T(8,128)}, f32[16,4,8,128]{3,2,1,0:T(8,128)}) custom-call(s32[4]{0:T(128)} %counts.3, f32[8,4,128]{2,1,0:T(4,128)} %particles_in.1), custom_call_target="tpu_custom_call" | custom-call | tf_op jit(solution)/shard_map/prepare/pallas_call | solution.py:220
  2.1 0.0 copy-start.2
  2.1 0.0 copy-start.3
  2.1 19.5 %all-to-all-start = ((f32[16,4,8,128]{3,2,1,0:T(8,128)}), f32[16,4,8,128]{3,2,1,0:T(8,128)S(1)}, u32[]{:S(2)}, u32[]{:S(2)}) async-start(f32[16,4,8,128]{3,2,1,0:T(8,128)} %get-tuple-element.22), calls=%async_computation | async-start | bytes 524288 | tf_op jit(solution)/shard_map/all_to_all | solution.py:234
  21.7 5.1 %collective-permute-start.1 = (f32[4,8,128]{2,1,0:T(8,128)}, f32[4,8,128]{2,1,0:T(8,128)S(1)}, u32[]{:S(2)}, u32[]{:S(2)}) collective-permute-start(f32[4,8,128]{2,1,0:T(8,128)} %get-tuple-element.21.own), channel_id=1, source_target_pairs={{128,0},{256,128},{384,256},{512,384},{640,512},{768,640},{896,768... | collective-permute-start | bytes 49160 | tf_op jit(solution)/shard_map/ppermute | solution.py:206
  26.8 1.9 %collective-permute-start = (f32[4,8,128]{2,1,0:T(8,128)}, f32[4,8,128]{2,1,0:T(8,128)S(1)}, u32[]{:S(2)}, u32[]{:S(2)}) collective-permute-start(f32[4,8,128]{2,1,0:T(8,128)} %get-tuple-element.21.own), channel_id=1, source_target_pairs={{0,128},{128,256},{256,384},{384,512},{512,640},{640,768},{768,896... | collective-permute-start | bytes 49160 | tf_op jit(solution)/shard_map/ppermute | solution.py:206
  28.7 0.0 collective-permute-done.1.down
  28.7 4.3 %collective-permute-done.up = f32[4,8,128]{2,1,0:T(8,128)S(1)} collective-permute-done((f32[4,8,128]{2,1,0:T(8,128)}, f32[4,8,128]{2,1,0:T(8,128)S(1)}, u32[]{:S(2)}, u32[]{:S(2)}) %collective-permute-start) | collective-permute-done | bytes 16416 | tf_op jit(solution)/shard_map/ppermute | solution.py:206
  33.0 0.7 copy-done
  33.7 2.4 %near.1 = (f32[4,128]{1,0:T(4,128)S(1)}, f32[4,3,128,128]{3,2,1,0:T(8,128)S(1)}, f32[4,3,128]{2,1,0:T(4,128)S(1)}) custom-call(f32[4,8,128]{2,1,0:T(8,128)S(1)} %copy-done, f32[4,8,128]{2,1,0:T(8,128)S(1)} %collective-permute-done.up, f32[4,8,128]{2,1,0:T(8,128)S(1)} %collective-permute-done.1.down), custom_call_target="tpu_custom_call" | custom-call | flops 11796480 | bytes 786432 | tf_op jit(solution)/shard_map/near/pallas_call | solution.py:236
  36.1 0.1 broadcast_in_dim.2
  36.3 13.6 %all_to_all.15 = f32[4,16,4,8,128]{4,3,2,1,0:T(8,128)S(1)} all-to-all(f32[4,16,4,8,128]{4,3,2,1,0:T(8,128)S(1)} %broadcast_in_dim.2), channel_id=1, replica_groups=mesh['slab'=8,'z'=16,'x'=4,'core'=2] {'x'}, dimensions={0} | all-to-all | bytes 2097152 | tf_op jit(solution)/shard_map/all_to_all | solution.py:247
  49.8 8.2 %collective-permute-start.2 = (f32[256,8,128]{2,1,0:T(8,128)S(1)}, f32[256,8,128]{2,1,0:T(8,128)S(1)}, u32[]{:S(2)}, u32[]{:S(2)}) collective-permute-start(f32[256,8,128]{2,1,0:T(8,128)S(1)} %bitcast.2), channel_id=1, source_target_pairs={{0,1},{1,0},{2,3},{3,2},{4,5},{5,4},{6,7},{7,6},{8,9},{9,8},{10,11... | collective-permute-start | bytes 3145736 | tf_op jit(solution)/shard_map/ppermute | solution.py:249
  58.1 2.3 %collective-permute-done.2.far = f32[256,8,128]{2,1,0:T(8,128)S(1)} collective-permute-done((f32[256,8,128]{2,1,0:T(8,128)S(1)}, f32[256,8,128]{2,1,0:T(8,128)S(1)}, u32[]{:S(2)}, u32[]{:S(2)}) %collective-permute-start.2) | collective-permute-done | bytes 1048608 | tf_op jit(solution)/shard_map/ppermute | solution.py:249
  60.3 3.8 %partner_density.1 = (f32[4,128]{1,0:T(4,128)}, f32[4,128]{1,0:T(4,128)S(1)}, f32[64,4,128]{2,1,0:T(4,128)}, f32[32,8,128]{2,1,0:T(8,128)S(1)}) custom-call(s32[4,8]{1,0:T(4,128)S(1)} %copy-done.2, s32[4]{0:T(128)S(1)} %copy-done.3, f32[4,8,128]{2,1,0:T(8,128)S(1)} %copy-done.1, f32[4,128]{1,0:T(4,128)S(1)} %get-tuple-element.26.part, ...), custom_call_target="tpu_custom_call" | custom-call | flops 10485760 | bytes 2097152 | tf_op jit(solution)/shard_map/partner_density/pallas_call | solution.py:250
  64.2 12.9 %all-to-all-start.2 = ((f32[64,4,128]{2,1,0:T(4,128)}), f32[64,4,128]{2,1,0:T(4,128)S(1)}, u32[]{:S(2)}, u32[]{:S(2)}) async-start(f32[64,4,128]{2,1,0:T(4,128)} %get-tuple-element.33), calls=%async_computation.2 | async-start | bytes 262144 | tf_op jit(solution)/shard_map/all_to_all | solution.py:266
  77.1 3.3 %collective-permute-start.4 = (f32[4,128]{1,0:T(4,128)S(1)}, f32[4,128]{1,0:T(4,128)S(1)}, u32[]{:S(2)}, u32[]{:S(2)}) collective-permute-start(f32[4,128]{1,0:T(4,128)S(1)} %get-tuple-element.35.mine), channel_id=1, source_target_pairs={{128,0},{256,128},{384,256},{512,384},{640,512},{768,640},{896,768... | collective-permute-start | bytes 6152 | tf_op jit(solution)/shard_map/ppermute | solution.py:206
  80.4 2.0 %collective-permute-start.3 = (f32[4,128]{1,0:T(4,128)S(1)}, f32[4,128]{1,0:T(4,128)S(1)}, u32[]{:S(2)}, u32[]{:S(2)}) collective-permute-start(f32[4,128]{1,0:T(4,128)S(1)} %get-tuple-element.35.mine), channel_id=1, source_target_pairs={{0,128},{128,256},{256,384},{384,512},{512,640},{640,768},{768,896... | collective-permute-start | bytes 6152 | tf_op jit(solution)/shard_map/ppermute | solution.py:206
  82.4 3.0 %factor.1 = (f32[4,8,128,128]{3,2,1,0:T(8,128)S(1)}, f32[4,3,128]{2,1,0:T(4,128)S(1)}) custom-call(f32[4,8,128]{2,1,0:T(8,128)S(1)} %copy-done.1, f32[32,8,128]{2,1,0:T(8,128)S(1)} %get-tuple-element.29.members), custom_call_target="tpu_custom_call" | custom-call | flops 20971520 | bytes 2097152 | tf_op jit(solution)/shard_map/factor/pallas_call | solution.py:267
  85.4 0.0 collective-permute-done.4.mine_down
  85.4 0.8 collective-permute-done.3.mine_up
  86.2 6.1 %all-to-all-done.2 = f32[64,4,128]{2,1,0:T(4,128)S(1)} async-done(((f32[64,4,128]{2,1,0:T(4,128)}), f32[64,4,128]{2,1,0:T(4,128)S(1)}, u32[]{:S(2)}, u32[]{:S(2)}) %all-to-all-start.2) | async-done | bytes 131104 | tf_op jit(solution)/shard_map/all_to_all | solution.py:266
  92.3 5.0 %all_gather.3.inverse = f32[512,128]{1,0:T(8,128)S(1)} all-gather(f32[256,128]{1,0:T(8,128)S(1)} %bitcast.4), channel_id=1, replica_groups=mesh['slab'=8,'z'=16,'x'=4,'core'=2] {'core'}, dimensions={0}, use_global_device_ids=true | all-gather | bytes 393216 | tf_op jit(solution)/shard_map/all_gather | solution.py:278
  97.3 4.0 %force.1 = f32[3,4,128]{2,1,0:T(4,128)} custom-call(s32[4,8]{1,0:T(4,128)S(1)} %copy-done.2, s32[4]{0:T(128)S(1)} %copy-done.3, f32[4,8,128]{2,1,0:T(8,128)S(1)} %copy-done.1, f32[4,8,128]{2,1,0:T(8,128)S(1)} %collective-permute-done.up, f32[4,8,128]{2,1,0:T(8,128)S(1)} %collective-permute-done.1.down, f32[32,8,128]{2,1,0:T(8,128)S(1)} %get-tuple-element.29.members, ...), custom_call_target="tpu_custom_call" | custom-call | flops 14417920 | bytes 2883584 | tf_op jit(solution)/shard_map/force/pallas_call | solution.py:279
  (6 shorter events, 0.0 us)
Async XLA Ops:
  2.1 58.2 %copy-start.1 = (f32[4,8,128]{2,1,0:T(8,128)S(1)}, f32[4,8,128]{2,1,0:T(8,128)}, u32[]{:S(2)}) copy-start(f32[4,8,128]{2,1,0:T(8,128)} %get-tuple-element.21.own) | copy-start | bytes 49156
  2.1 58.2 %copy-start.2 = (s32[4,8]{1,0:T(4,128)S(1)}, s32[4,8]{1,0:T(4,128)}, u32[]{:S(2)}) copy-start(s32[4,8]{1,0:T(4,128)} %partners.3) | copy-start | bytes 388
  2.1 58.2 %copy-start.3 = (s32[4]{0:T(128)S(1)}, s32[4]{0:T(128)}, u32[]{:S(2)}) copy-start(s32[4]{0:T(128)} %counts.3) | copy-start | bytes 52
  2.1 34.0 %all-to-all-start = ((f32[16,4,8,128]{3,2,1,0:T(8,128)}), f32[16,4,8,128]{3,2,1,0:T(8,128)S(1)}, u32[]{:S(2)}, u32[]{:S(2)}) async-start(f32[16,4,8,128]{3,2,1,0:T(8,128)} %get-tuple-element.22), calls=%async_computation | async-start | bytes 524288 | tf_op jit(solution)/shard_map/all_to_all | solution.py:234
  21.7 7.0 %collective-permute-start.1 = (f32[4,8,128]{2,1,0:T(8,128)}, f32[4,8,128]{2,1,0:T(8,128)S(1)}, u32[]{:S(2)}, u32[]{:S(2)}) collective-permute-start(f32[4,8,128]{2,1,0:T(8,128)} %get-tuple-element.21.own), channel_id=1, source_target_pairs={{128,0},{256,128},{384,256},{512,384},{640,512},{768,640},{896,768... | collective-permute-start | bytes 49160 | tf_op jit(solution)/shard_map/ppermute | solution.py:206
  26.8 6.2 %collective-permute-start = (f32[4,8,128]{2,1,0:T(8,128)}, f32[4,8,128]{2,1,0:T(8,128)S(1)}, u32[]{:S(2)}, u32[]{:S(2)}) collective-permute-start(f32[4,8,128]{2,1,0:T(8,128)} %get-tuple-element.21.own), channel_id=1, source_target_pairs={{0,128},{128,256},{256,384},{384,512},{512,640},{640,768},{768,896... | collective-permute-start | bytes 49160 | tf_op jit(solution)/shard_map/ppermute | solution.py:206
  33.0 0.7 copy-start
  49.8 10.5 %collective-permute-start.2 = (f32[256,8,128]{2,1,0:T(8,128)S(1)}, f32[256,8,128]{2,1,0:T(8,128)S(1)}, u32[]{:S(2)}, u32[]{:S(2)}) collective-permute-start(f32[256,8,128]{2,1,0:T(8,128)S(1)} %bitcast.2), channel_id=1, source_target_pairs={{0,1},{1,0},{2,3},{3,2},{4,5},{5,4},{6,7},{7,6},{8,9},{9,8},{10,11... | collective-permute-start | bytes 3145736 | tf_op jit(solution)/shard_map/ppermute | solution.py:249
  64.2 28.2 %all-to-all-start.2 = ((f32[64,4,128]{2,1,0:T(4,128)}), f32[64,4,128]{2,1,0:T(4,128)S(1)}, u32[]{:S(2)}, u32[]{:S(2)}) async-start(f32[64,4,128]{2,1,0:T(4,128)} %get-tuple-element.33), calls=%async_computation.2 | async-start | bytes 262144 | tf_op jit(solution)/shard_map/all_to_all | solution.py:266
  77.1 8.3 %collective-permute-start.4 = (f32[4,128]{1,0:T(4,128)S(1)}, f32[4,128]{1,0:T(4,128)S(1)}, u32[]{:S(2)}, u32[]{:S(2)}) collective-permute-start(f32[4,128]{1,0:T(4,128)S(1)} %get-tuple-element.35.mine), channel_id=1, source_target_pairs={{128,0},{256,128},{384,256},{512,384},{640,512},{768,640},{896,768... | collective-permute-start | bytes 6152 | tf_op jit(solution)/shard_map/ppermute | solution.py:206
  80.4 5.8 %collective-permute-start.3 = (f32[4,128]{1,0:T(4,128)S(1)}, f32[4,128]{1,0:T(4,128)S(1)}, u32[]{:S(2)}, u32[]{:S(2)}) collective-permute-start(f32[4,128]{1,0:T(4,128)S(1)} %get-tuple-element.35.mine), channel_id=1, source_target_pairs={{0,128},{128,256},{256,384},{384,512},{512,640},{640,768},{768,896... | collective-permute-start | bytes 6152 | tf_op jit(solution)/shard_map/ppermute | solution.py:206

commit v6 on v5

--- a/solution.py
+++ b/solution.py
@@ -107,20 +107,54 @@
     lax.fori_loop(0, BINS, per_bin, 0)
 
 
-def partner_density_kernel(partners, counts, own, part, near, far, den_out, inv_out, block, members, tall, acc):
-    me = lax.axis_index("core")
-
+def place(bin_id):
+    index = (((bin_id >> 3) & 3) * 16 + (bin_id >> 5)) * BINS + (bin_id & 3)
+    return index, ((bin_id >> 2) & 1) == lax.axis_index("core")
+
+
+def add_partners(partners, b, held, wanted, cols, sums):
+    for k in range(LINKS):
+        index, local = place(partners[b, k])
+
+        @pl.when(local == wanted)
+        def _():
+            row = reader(held, index)
+            for c in range(CHUNKS):
+                part = slice(c * 8, c * 8 + 8)
+                dx = cols[b, 0, part, :] - row(0)
+                dy = cols[b, 1, part, :] - row(1)
+                dz = cols[b, 2, part, :] - row(2)
+                s = jnp.maximum(1.0 - root(dx * dx + dy * dy + dz * dz) * cols[b, 3, part, :], 0.0)
+                s2 = s * s
+                sums[b, part, :] = sums[b, part, :] + (s2 * s2) * (5.0 - 4.0 * s) * row(7)
+
+
+def local_density_kernel(partners, own, near, cols, sums, tall):
+    def per_bin(b, carry):
+        tall[...] = own[b].T
+        for c in range(CHUNKS):
+            part = slice(c * 8, c * 8 + 8)
+            xi, yi, zi, hi = columns(tall, c, (0, 1, 2, 6))
+            for r, value in enumerate((xi, yi, zi, 0.5 / hi)):
+                cols[b, r, part, :] = value
+            sums[b, part, :] = jnp.zeros((8, SLOTS), F32)
+        add_partners(partners, b, near, True, cols, sums)
+        return carry
+
+    lax.fori_loop(0, BINS, per_bin, 0)
+
+
+def partner_density_kernel(partners, own, part, near, far, cols, start, den_out, inv_out, block, members, sums):
     def per_bin(b, carry):
         for k in range(LINKS):
-            bin_id = partners[b, k]
-            index = (((bin_id >> 3) & 3) * 16 + (bin_id >> 5)) * BINS + (bin_id & 3)
-            mine = ((bin_id >> 2) & 1) == me
-            members[b * LINKS + k] = jnp.where(mine, near[index], far[index])
-        tall[...] = own[b].T
-        far_part = density_terms(tall, [reader(members, b * LINKS + k) for k in range(LINKS)], acc)
+            index, local = place(partners[b, k])
+            members[b * LINKS + k] = jnp.where(local, near[index], far[index])
+        sums[b] = start[b]
+        add_partners(partners, b, far, False, cols, sums)
+        width = own[b, 6:7, :]
+        far_part = jnp.sum(sums[b].T, axis=0, keepdims=True) * (weight_norm / (width * width * width))
         raw = part[pl.ds(b, 1), :] + far_part
-        lane = lax.broadcasted_iota(jnp.int32, (1, SLOTS), 1)
-        filled = (lane < counts[b]).astype(F32)
+        filled = (own[b, 7:8, :] > 0.0).astype(F32)
         den_out[pl.ds(b, 1), :] = filled * raw
         inv_out[pl.ds(b, 1), :] = 1.0 / (filled * raw + (1.0 - filled))
         return carry
@@ -131,7 +165,9 @@
         block[copy] = inverse
 
 
-def factor_kernel(own, members, factors, base, tall, acc3):
+def factor_kernel(own, members, density, den_out, factors, base, tall, acc3):
+    den_out[...] = density[...]
+
     def per_bin(b, carry):
         tall[...] = own[b].T
         others = [reader(members, b * LINKS + k) for k in range(LINKS)]
@@ -144,7 +180,6 @@
 
 def force_kernel(
     partners,
-    counts,
     own,
     up,
     down,
@@ -186,8 +221,7 @@
                 bz = bz + factor * (wi - row(5))
             for d, total in enumerate((ax, ay, az, bx, by, bz)):
                 acc[d, c * 8 : c * 8 + 8, :] = total
-        lane = lax.broadcasted_iota(jnp.int32, (1, SLOTS), 1)
-        scale = (lane < counts[b]).astype(F32) * (32.0 * force_norm)
+        scale = (own[b, 7:8, :] > 0.0).astype(F32) * (32.0 * force_norm)
         weight = weights[0:1, :]
         for d in range(3):
             push = jnp.sum(acc[d].T, axis=0, keepdims=True)
@@ -216,7 +250,7 @@
 
 
 def per_device(particles, counts, partners):
-    layers, cols = lax.axis_size("z"), lax.axis_size("x")
+    layers, cols_count = lax.axis_size("z"), lax.axis_size("x")
     own, block = pl.pallas_call(
         prepare_kernel,
         out_shape=(shape(BINS, ROWS, SLOTS), shape(layers, BINS, ROWS, SLOTS)),
@@ -244,42 +278,56 @@
         name="near",
     )(own, up, down)
     column, part, near_factors, near_base = lax.optimization_barrier((column, part, near_factors, near_base))
-    near = lax.all_to_all(jnp.broadcast_to(column[None], (cols,) + column.shape), "x", 0, 0, tiled=True)
+    near = lax.all_to_all(jnp.broadcast_to(column[None], (cols_count,) + column.shape), "x", 0, 0, tiled=True)
     near = near.reshape(-1, ROWS, SLOTS)
     far = lax.ppermute(near, "core", [(0, 1), (1, 0)])
+    cols, sums = pl.pallas_call(
+        local_density_kernel,
+        out_shape=(shape(BINS, 4, SLOTS, SLOTS), shape(BINS, SLOTS, SLOTS)),
+        in_specs=[SMEM] + [VMEM] * 2,
+        out_specs=(VMEM,) * 2,
+        scratch_shapes=[tall],
+        cost_estimate=cost(LINKS * BINS, 20),
+        compiler_params=limit(8),
+        name="local_density",
+    )(partners, own, near)
     density, mine, block, members = pl.pallas_call(
         partner_density_kernel,
         out_shape=(
             shape(BINS, SLOTS),
             shape(BINS, SLOTS),
-            shape(layers * cols, BINS, SLOTS),
+            shape(layers * cols_count, BINS, SLOTS),
             shape(BINS * LINKS, ROWS, SLOTS),
         ),
-        in_specs=[SMEM, SMEM] + [VMEM] * 4,
+        in_specs=[SMEM] + [VMEM] * 6,
         out_specs=(VMEM,) * 4,
-        scratch_shapes=[tall, acc],
+        scratch_shapes=[pltpu.VMEM((BINS, SLOTS, SLOTS), F32)],
         cost_estimate=cost(LINKS * BINS, 20),
         compiler_params=limit(8),
         name="partner_density",
-    )(partners, counts, own, part, near, far)
+    )(partners, own, part, near, far, cols, sums)
     mine_up, mine_down = both_ways(mine)
     inverse = lax.all_to_all(block, ("z", "x"), 0, 0, tiled=True)
-    far_factors, far_base = pl.pallas_call(
+    density, far_factors, far_base = pl.pallas_call(
         factor_kernel,
-        out_shape=(shape(BINS, LINKS, SLOTS, SLOTS), shape(BINS, 3, SLOTS)),
-        in_specs=[VMEM] * 2,
-        out_specs=(VMEM,) * 2,
+        out_shape=(
+            shape(BINS, SLOTS),
+            shape(BINS, LINKS, SLOTS, SLOTS),
+            shape(BINS, 3, SLOTS),
+        ),
+        in_specs=[VMEM] * 3,
+        out_specs=(VMEM,) * 3,
         scratch_shapes=[tall, acc3],
         cost_estimate=cost(LINKS * BINS, 40),
         compiler_params=limit(8),
         name="factor",
-    )(own, members)
+    )(own, members, density)
     inverse, far_base, mine_up, mine_down = lax.optimization_barrier((inverse, far_base, mine_up, mine_down))
     inverse = lax.all_gather(inverse.reshape(-1, SLOTS), "core", axis=0, tiled=True)
     acceleration = pl.pallas_call(
         force_kernel,
         out_shape=shape(3, BINS, SLOTS),
-        in_specs=[SMEM, SMEM] + [VMEM] * 12,
+        in_specs=[SMEM] + [VMEM] * 12,
         out_specs=VMEM,
         scratch_shapes=[pltpu.VMEM((16, SLOTS), F32), tall, pltpu.VMEM((6, SLOTS, SLOTS), F32)],
         cost_estimate=cost(COUNT * BINS, 20),
@@ -287,7 +335,6 @@
         name="force",
     )(
         partners,
-        counts,
         own,
         up,
         down,

time: 102 us -> 102 us (level)
  Pallas kernels: 14.8 us -> 16.9 us
  waiting for transfers between devices: 13.4 us -> 11.6 us
    pallas_call x1 -> x2, Pallas kernels: 3.01 us -> 5.66 us  [the longest x1 3.09 us: per_device(): pl.pallas_call(factor_kernel, out_shape=(shape(BINS, SLOTS), shape(BINS,...]
    ppermute x1, waiting for transfers between devices: 2.26 us -> 0.01 us  [per_device(): far = lax.ppermute(near, 'core', [(0, 1), (1, 0)])]
  transfers between devices with their start and end apart: 7 -> 7, of which waited for: 4 -> 3; matrix products, arithmetic and copies ran while one was open for 0% -> 0% of each run, Pallas kernels for 5% -> 8%
where the time goes in v6:
time: 102 us; the launch traced here: 101 us
  starting transfers between devices  52.9 us (52%)
  blocking collectives  18 us (18%)
  Pallas kernels  16.9 us (17%)
  waiting for transfers between devices  11.6 us (11%)
    all_to_all x1, starting transfers between devices, per_device(): column = lax.all_to_all(block, 'z', 0, 0, tiled=True)  19.4 us
    all_to_all x1, blocking collectives, per_device(): lax.all_to_all(jnp.broadcast_to(column[None], (cols_count,) + column.shap...  13.6 us
    all_to_all x1, starting transfers between devices, per_device(): inverse = lax.all_to_all(block, ('z', 'x'), 0, 0, tiled=True)  13 us
    ppermute x4, starting transfers between devices, both_ways(): return (lax.ppermute(value, 'slab', up), lax.ppermute(value, 'slab', down))  12.3 us
    ppermute x1, starting transfers between devices, per_device(): far = lax.ppermute(near, 'core', [(0, 1), (1, 0)])  8.22 us
    all_to_all x1, waiting for transfers between devices, per_device(): inverse = lax.all_to_all(block, ('z', 'x'), 0, 0, tiled=True)  6.64 us
    ppermute x4, waiting for transfers between devices, both_ways(): return (lax.ppermute(value, 'slab', up), lax.ppermute(value, 'slab', down))  4.99 us
    all_gather x1, blocking collectives, per_device(): lax.all_gather(inverse.reshape(-1, SLOTS), 'core', axis=0, tiled=True)  4.46 us
  transfers between devices with their start and end apart: 7, of which 3 were waited for; matrix products, arithmetic and copies ran while one was open for 0% of the time, Pallas kernels for 8%

profile of v6, /device:TPU:1, one launch (start us, length us, event | category | flops | bytes accessed | tf_op | source)
XLA Modules:
  0.0 101.1 jit_solution(10679653262563450072)
XLA Ops:
  0.6 1.5 %prepare.1 = (f32[4,8,128]{2,1,0:T(8,128)}, f32[16,4,8,128]{3,2,1,0:T(8,128)}) custom-call(s32[4]{0:T(128)} %counts_in.1, f32[8,4,128]{2,1,0:T(4,128)} %particles_in.1), custom_call_target="tpu_custom_call" | custom-call | tf_op jit(solution)/shard_map/prepare/pallas_call | solution.py:254
  2.1 0.0 copy-start.2
  2.1 19.4 %all-to-all-start = ((f32[16,4,8,128]{3,2,1,0:T(8,128)}), f32[16,4,8,128]{3,2,1,0:T(8,128)S(1)}, u32[]{:S(2)}, u32[]{:S(2)}) async-start(f32[16,4,8,128]{3,2,1,0:T(8,128)} %get-tuple-element.25), calls=%async_computation | async-start | bytes 524288 | tf_op jit(solution)/shard_map/all_to_all | solution.py:268
  21.6 5.1 %collective-permute-start.1 = (f32[4,8,128]{2,1,0:T(8,128)}, f32[4,8,128]{2,1,0:T(8,128)S(1)}, u32[]{:S(2)}, u32[]{:S(2)}) collective-permute-start(f32[4,8,128]{2,1,0:T(8,128)} %get-tuple-element.24.own), channel_id=1, source_target_pairs={{128,0},{256,128},{384,256},{512,384},{640,512},{768,640},{896,768... | collective-permute-start | bytes 49160 | tf_op jit(solution)/shard_map/ppermute | solution.py:240
  26.7 1.9 %collective-permute-start = (f32[4,8,128]{2,1,0:T(8,128)}, f32[4,8,128]{2,1,0:T(8,128)S(1)}, u32[]{:S(2)}, u32[]{:S(2)}) collective-permute-start(f32[4,8,128]{2,1,0:T(8,128)} %get-tuple-element.24.own), channel_id=1, source_target_pairs={{0,128},{128,256},{256,384},{384,512},{512,640},{640,768},{768,896... | collective-permute-start | bytes 49160 | tf_op jit(solution)/shard_map/ppermute | solution.py:240
  28.6 0.0 collective-permute-done.1.down
  28.6 4.3 %collective-permute-done.up = f32[4,8,128]{2,1,0:T(8,128)S(1)} collective-permute-done((f32[4,8,128]{2,1,0:T(8,128)}, f32[4,8,128]{2,1,0:T(8,128)S(1)}, u32[]{:S(2)}, u32[]{:S(2)}) %collective-permute-start) | collective-permute-done | bytes 16416 | tf_op jit(solution)/shard_map/ppermute | solution.py:240
  32.9 0.7 copy-done
  33.6 2.4 %near.1 = (f32[4,128]{1,0:T(4,128)S(1)}, f32[4,3,128,128]{3,2,1,0:T(8,128)S(1)}, f32[4,3,128]{2,1,0:T(4,128)S(1)}) custom-call(f32[4,8,128]{2,1,0:T(8,128)S(1)} %copy-done, f32[4,8,128]{2,1,0:T(8,128)S(1)} %collective-permute-done.up, f32[4,8,128]{2,1,0:T(8,128)S(1)} %collective-permute-done.1.down), custom_call_target="tpu_custom_call" | custom-call | flops 11796480 | bytes 786432 | tf_op jit(solution)/shard_map/near/pallas_call | solution.py:270
  36.0 0.0 all-to-all-done
  36.0 0.1 broadcast_in_dim.2
  36.1 13.6 %all_to_all.15 = f32[4,16,4,8,128]{4,3,2,1,0:T(8,128)S(1)} all-to-all(f32[4,16,4,8,128]{4,3,2,1,0:T(8,128)S(1)} %broadcast_in_dim.2), channel_id=1, replica_groups=mesh['slab'=8,'z'=16,'x'=4,'core'=2] {'x'}, dimensions={0} | all-to-all | bytes 2097152 | tf_op jit(solution)/shard_map/all_to_all | solution.py:281
  49.7 8.2 %collective-permute-start.2 = (f32[256,8,128]{2,1,0:T(8,128)S(1)}, f32[256,8,128]{2,1,0:T(8,128)S(1)}, u32[]{:S(2)}, u32[]{:S(2)}) collective-permute-start(f32[256,8,128]{2,1,0:T(8,128)S(1)} %bitcast.2), channel_id=1, source_target_pairs={{0,1},{1,0},{2,3},{3,2},{4,5},{5,4},{6,7},{7,6},{8,9},{9,8},{10,11... | collective-permute-start | bytes 3145736 | tf_op jit(solution)/shard_map/ppermute | solution.py:283
  57.9 2.6 %local_density.1 = (f32[4,4,128,128]{3,2,1,0:T(8,128)S(1)}, f32[4,128,128]{2,1,0:T(8,128)S(1)}) custom-call(s32[4,8]{1,0:T(4,128)S(1)} %copy-done.2, f32[4,8,128]{2,1,0:T(8,128)S(1)} %copy-done.1, f32[256,8,128]{2,1,0:T(8,128)S(1)} %bitcast.3), custom_call_target="tpu_custom_call" | custom-call | flops 10485760 | bytes 2097152 | tf_op jit(solution)/shard_map/local_density/pallas_call | solution.py:284
  60.5 3.3 %partner_density.1 = (f32[4,128]{1,0:T(4,128)S(1)}, f32[4,128]{1,0:T(4,128)S(1)}, f32[64,4,128]{2,1,0:T(4,128)}, f32[32,8,128]{2,1,0:T(8,128)S(1)}) custom-call(s32[4,8]{1,0:T(4,128)S(1)} %copy-done.2, f32[4,8,128]{2,1,0:T(8,128)S(1)} %copy-done.1, f32[4,128]{1,0:T(4,128)S(1)} %get-tuple-element.29.part, f32[256,8,128]{2,1,0:T(8,128)S(1)} %bitcast.4, ...), custom_call_target="tpu_custom_call" | custom-call | flops 10485760 | bytes 2097152 | tf_op jit(solution)/shard_map/partner_density/pallas_call | solution.py:294
  63.8 13.0 %all-to-all-start.2 = ((f32[64,4,128]{2,1,0:T(4,128)}), f32[64,4,128]{2,1,0:T(4,128)S(1)}, u32[]{:S(2)}, u32[]{:S(2)}) async-start(f32[64,4,128]{2,1,0:T(4,128)} %get-tuple-element.39), calls=%async_computation.2 | async-start | bytes 262144 | tf_op jit(solution)/shard_map/all_to_all | solution.py:310
  76.8 3.3 %collective-permute-start.4 = (f32[4,128]{1,0:T(4,128)S(1)}, f32[4,128]{1,0:T(4,128)S(1)}, u32[]{:S(2)}, u32[]{:S(2)}) collective-permute-start(f32[4,128]{1,0:T(4,128)S(1)} %get-tuple-element.41.mine), channel_id=1, source_target_pairs={{128,0},{256,128},{384,256},{512,384},{640,512},{768,640},{896,768... | collective-permute-start | bytes 6152 | tf_op jit(solution)/shard_map/ppermute | solution.py:240
  80.1 2.0 %collective-permute-start.3 = (f32[4,128]{1,0:T(4,128)S(1)}, f32[4,128]{1,0:T(4,128)S(1)}, u32[]{:S(2)}, u32[]{:S(2)}) collective-permute-start(f32[4,128]{1,0:T(4,128)S(1)} %get-tuple-element.41.mine), channel_id=1, source_target_pairs={{0,128},{128,256},{256,384},{384,512},{512,640},{640,768},{768,896... | collective-permute-start | bytes 6152 | tf_op jit(solution)/shard_map/ppermute | solution.py:240
  82.1 3.1 %factor.1 = (f32[4,128]{1,0:T(4,128)}, f32[4,8,128,128]{3,2,1,0:T(8,128)S(1)}, f32[4,3,128]{2,1,0:T(4,128)S(1)}) custom-call(f32[4,8,128]{2,1,0:T(8,128)S(1)} %copy-done.1, f32[32,8,128]{2,1,0:T(8,128)S(1)} %get-tuple-element.33.members, f32[4,128]{1,0:T(4,128)S(1)} %get-tuple-element.34.density), custom_call_target="tpu_custom_call" | custom-call | flops 20971520 | bytes 2097152 | tf_op jit(solution)/shard_map/factor/pallas_call | solution.py:311
  85.2 0.0 collective-permute-done.4.mine_down
  85.2 0.7 collective-permute-done.3.mine_up
  85.9 6.6 %all-to-all-done.2 = f32[64,4,128]{2,1,0:T(4,128)S(1)} async-done(((f32[64,4,128]{2,1,0:T(4,128)}), f32[64,4,128]{2,1,0:T(4,128)S(1)}, u32[]{:S(2)}, u32[]{:S(2)}) %all-to-all-start.2) | async-done | bytes 131104 | tf_op jit(solution)/shard_map/all_to_all | solution.py:310
  92.5 4.5 %all_gather.3.inverse = f32[512,128]{1,0:T(8,128)S(1)} all-gather(f32[256,128]{1,0:T(8,128)S(1)} %bitcast.5), channel_id=1, replica_groups=mesh['slab'=8,'z'=16,'x'=4,'core'=2] {'core'}, dimensions={0}, use_global_device_ids=true | all-gather | bytes 393216 | tf_op jit(solution)/shard_map/all_gather | solution.py:326
  97.0 4.1 %force.1 = f32[3,4,128]{2,1,0:T(4,128)} custom-call(s32[4,8]{1,0:T(4,128)S(1)} %copy-done.2, f32[4,8,128]{2,1,0:T(8,128)S(1)} %copy-done.1, f32[4,8,128]{2,1,0:T(8,128)S(1)} %collective-permute-done.up, f32[4,8,128]{2,1,0:T(8,128)S(1)} %collective-permute-done.1.down, f32[32,8,128]{2,1,0:T(8,128)S(1)} %get-tuple-element.33.members, ...), custom_call_target="tpu_custom_call" | custom-call | flops 14417920 | bytes 2883584 | tf_op jit(solution)/shard_map/force/pallas_call | solution.py:327
  (5 shorter events, 0.0 us)
Async XLA Ops:
  2.1 55.8 %copy-start.1 = (f32[4,8,128]{2,1,0:T(8,128)S(1)}, f32[4,8,128]{2,1,0:T(8,128)}, u32[]{:S(2)}) copy-start(f32[4,8,128]{2,1,0:T(8,128)} %get-tuple-element.24.own) | copy-start | bytes 49156
  2.1 55.8 %copy-start.2 = (s32[4,8]{1,0:T(4,128)S(1)}, s32[4,8]{1,0:T(4,128)}, u32[]{:S(2)}) copy-start(s32[4,8]{1,0:T(4,128)} %partners.5) | copy-start | bytes 388
  2.1 33.9 %all-to-all-start = ((f32[16,4,8,128]{3,2,1,0:T(8,128)}), f32[16,4,8,128]{3,2,1,0:T(8,128)S(1)}, u32[]{:S(2)}, u32[]{:S(2)}) async-start(f32[16,4,8,128]{3,2,1,0:T(8,128)} %get-tuple-element.25), calls=%async_computation | async-start | bytes 524288 | tf_op jit(solution)/shard_map/all_to_all | solution.py:268
  21.6 7.0 %collective-permute-start.1 = (f32[4,8,128]{2,1,0:T(8,128)}, f32[4,8,128]{2,1,0:T(8,128)S(1)}, u32[]{:S(2)}, u32[]{:S(2)}) collective-permute-start(f32[4,8,128]{2,1,0:T(8,128)} %get-tuple-element.24.own), channel_id=1, source_target_pairs={{128,0},{256,128},{384,256},{512,384},{640,512},{768,640},{896,768... | collective-permute-start | bytes 49160 | tf_op jit(solution)/shard_map/ppermute | solution.py:240
  26.7 6.2 %collective-permute-start = (f32[4,8,128]{2,1,0:T(8,128)}, f32[4,8,128]{2,1,0:T(8,128)S(1)}, u32[]{:S(2)}, u32[]{:S(2)}) collective-permute-start(f32[4,8,128]{2,1,0:T(8,128)} %get-tuple-element.24.own), channel_id=1, source_target_pairs={{0,128},{128,256},{256,384},{384,512},{512,640},{640,768},{768,896... | collective-permute-start | bytes 49160 | tf_op jit(solution)/shard_map/ppermute | solution.py:240
  32.9 0.7 copy-start
  49.7 10.8 %collective-permute-start.2 = (f32[256,8,128]{2,1,0:T(8,128)S(1)}, f32[256,8,128]{2,1,0:T(8,128)S(1)}, u32[]{:S(2)}, u32[]{:S(2)}) collective-permute-start(f32[256,8,128]{2,1,0:T(8,128)S(1)} %bitcast.2), channel_id=1, source_target_pairs={{0,1},{1,0},{2,3},{3,2},{4,5},{5,4},{6,7},{7,6},{8,9},{9,8},{10,11... | collective-permute-start | bytes 3145736 | tf_op jit(solution)/shard_map/ppermute | solution.py:283
  63.8 28.7 %all-to-all-start.2 = ((f32[64,4,128]{2,1,0:T(4,128)}), f32[64,4,128]{2,1,0:T(4,128)S(1)}, u32[]{:S(2)}, u32[]{:S(2)}) async-start(f32[64,4,128]{2,1,0:T(4,128)} %get-tuple-element.39), calls=%async_computation.2 | async-start | bytes 262144 | tf_op jit(solution)/shard_map/all_to_all | solution.py:310
  76.8 8.4 %collective-permute-start.4 = (f32[4,128]{1,0:T(4,128)S(1)}, f32[4,128]{1,0:T(4,128)S(1)}, u32[]{:S(2)}, u32[]{:S(2)}) collective-permute-start(f32[4,128]{1,0:T(4,128)S(1)} %get-tuple-element.41.mine), channel_id=1, source_target_pairs={{128,0},{256,128},{384,256},{512,384},{640,512},{768,640},{896,768... | collective-permute-start | bytes 6152 | tf_op jit(solution)/shard_map/ppermute | solution.py:240
  80.1 5.8 %collective-permute-start.3 = (f32[4,128]{1,0:T(4,128)S(1)}, f32[4,128]{1,0:T(4,128)S(1)}, u32[]{:S(2)}, u32[]{:S(2)}) collective-permute-start(f32[4,128]{1,0:T(4,128)S(1)} %get-tuple-element.41.mine), channel_id=1, source_target_pairs={{0,128},{128,256},{256,384},{384,512},{512,640},{640,768},{768,896... | collective-permute-start | bytes 6152 | tf_op jit(solution)/shard_map/ppermute | solution.py:240

commit v7 on v6

--- a/solution.py
+++ b/solution.py
@@ -178,56 +178,57 @@
     lax.fori_loop(0, BINS, per_bin, 0)
 
 
-def force_kernel(
-    partners,
-    own,
-    up,
-    down,
-    members,
-    near_factors,
-    far_factors,
-    near_base,
-    far_base,
-    mine,
-    mine_up,
-    mine_down,
-    inverse,
-    out,
-    weights,
-    tall,
-    acc,
-):
-    def per_bin(b, carry):
-        for j, ref in enumerate((mine, mine_up, mine_down)):
-            weights[j : j + 1, :] = ref[pl.ds(b, 1), :]
+def force_terms(b, tall, others, acc):
+    for c in range(CHUNKS):
+        part = slice(c * 8, c * 8 + 8)
+        xi, yi, zi, ui, vi, wi = columns(tall, c, range(6))
+        ax = jnp.zeros((8, SLOTS), F32)
+        ay, az, bx, by, bz = (ax,) * 5
+        for row, factors, at, weight in others:
+            factor = factors[b, at, part, :] * weight()
+            ax = ax + factor * (xi - row(0))
+            ay = ay + factor * (yi - row(1))
+            az = az + factor * (zi - row(2))
+            bx = bx + factor * (ui - row(3))
+            by = by + factor * (vi - row(4))
+            bz = bz + factor * (wi - row(5))
+        for d, total in enumerate((ax, ay, az, bx, by, bz)):
+            acc[d, part, :] = total
+    return [jnp.sum(acc[d].T, axis=0, keepdims=True) for d in range(6)]
+
+
+def spread_row(ref, j):
+    return lambda: ref[pl.ds(j, 8, stride=0), :]
+
+
+def near_force_kernel(own, up, down, factors, near_base, far_base, mine, mine_up, mine_down, out, tall, acc):
+    def per_bin(b, carry):
+        tall[...] = own[b].T
+        pairs = ((own, mine), (up, mine_up), (down, mine_down))
+        others = [(reader(ref, b), factors, j, spread_row(weight, b)) for j, (ref, weight) in enumerate(pairs)]
+        sums = force_terms(b, tall, others, acc)
+        weight = mine[pl.ds(b, 1), :]
+        for d in range(3):
+            still = near_base[b, d : d + 1, :] + far_base[b, d : d + 1, :]
+            out[b, d : d + 1, :] = sums[d] + weight * (still - viscosity * sums[3 + d])
+        return carry
+
+    lax.fori_loop(0, BINS, per_bin, 0)
+
+
+def force_kernel(partners, own, members, factors, begun, mine, inverse, out, weights, tall, acc):
+    def per_bin(b, carry):
         for k in range(LINKS):
             bin_id = partners[b, k]
             at = ((bin_id >> 2) & 1) * 256 + (bin_id >> 3) * BINS + (bin_id & 3)
-            weights[3 + k : 4 + k, :] = inverse[pl.ds(at, 1), :]
-        tall[...] = own[b].T
-        others = [(reader(ref, b), near_factors, j) for j, ref in enumerate((own, up, down))]
-        others += [(reader(members, b * LINKS + k), far_factors, k) for k in range(LINKS)]
-        for c in range(CHUNKS):
-            xi, yi, zi, ui, vi, wi = columns(tall, c, range(6))
-            ax = jnp.zeros((8, SLOTS), F32)
-            ay, az, bx, by, bz = (ax,) * 5
-            for j, (row, factors, at) in enumerate(others):
-                factor = factors[b, at, c * 8 : c * 8 + 8, :] * weights[pl.ds(j, 8, stride=0), :]
-                ax = ax + factor * (xi - row(0))
-                ay = ay + factor * (yi - row(1))
-                az = az + factor * (zi - row(2))
-                bx = bx + factor * (ui - row(3))
-                by = by + factor * (vi - row(4))
-                bz = bz + factor * (wi - row(5))
-            for d, total in enumerate((ax, ay, az, bx, by, bz)):
-                acc[d, c * 8 : c * 8 + 8, :] = total
+            weights[k : k + 1, :] = inverse[pl.ds(at, 1), :]
+        tall[...] = own[b].T
+        others = [(reader(members, b * LINKS + k), factors, k, spread_row(weights, k)) for k in range(LINKS)]
+        sums = force_terms(b, tall, others, acc)
         scale = (own[b, 7:8, :] > 0.0).astype(F32) * (32.0 * force_norm)
-        weight = weights[0:1, :]
+        drag = viscosity * mine[pl.ds(b, 1), :]
         for d in range(3):
-            push = jnp.sum(acc[d].T, axis=0, keepdims=True)
-            drag = jnp.sum(acc[3 + d].T, axis=0, keepdims=True)
-            still = near_base[b, d : d + 1, :] + far_base[b, d : d + 1, :]
-            out[d, pl.ds(b, 1), :] = (push + weight * (still - viscosity * drag)) * scale
+            out[d, pl.ds(b, 1), :] = (begun[b, d : d + 1, :] + sums[d] - drag * sums[3 + d]) * scale
         return carry
 
     lax.fori_loop(0, BINS, per_bin, 0)
@@ -322,32 +323,29 @@
         compiler_params=limit(8),
         name="factor",
     )(own, members, density)
-    inverse, far_base, mine_up, mine_down = lax.optimization_barrier((inverse, far_base, mine_up, mine_down))
+    acc6 = pltpu.VMEM((6, SLOTS, SLOTS), F32)
+    begun = pl.pallas_call(
+        near_force_kernel,
+        out_shape=shape(BINS, 3, SLOTS),
+        in_specs=[VMEM] * 9,
+        out_specs=VMEM,
+        scratch_shapes=[tall, acc6],
+        cost_estimate=cost(3 * BINS, 40),
+        compiler_params=limit(8),
+        name="near_force",
+    )(own, up, down, near_factors, near_base, far_base, mine, mine_up, mine_down)
+    inverse, begun = lax.optimization_barrier((inverse, begun))
     inverse = lax.all_gather(inverse.reshape(-1, SLOTS), "core", axis=0, tiled=True)
     acceleration = pl.pallas_call(
         force_kernel,
         out_shape=shape(3, BINS, SLOTS),
-        in_specs=[SMEM] + [VMEM] * 12,
+        in_specs=[SMEM] + [VMEM] * 6,
         out_specs=VMEM,
-        scratch_shapes=[pltpu.VMEM((16, SLOTS), F32), tall, pltpu.VMEM((6, SLOTS, SLOTS), F32)],
-        cost_estimate=cost(COUNT * BINS, 20),
+        scratch_shapes=[pltpu.VMEM((8, SLOTS), F32), tall, acc6],
+        cost_estimate=cost(LINKS * BINS, 20),
         compiler_params=limit(8),
         name="force",
-    )(
-        partners,
-        own,
-        up,
-        down,
-        members,
-        near_factors,
-        far_factors,
-        near_base,
-        far_base,
-        mine,
-        mine_up,
-        mine_down,
-        inverse,
-    )
+    )(partners, own, members, far_factors, begun, mine, inverse)
     return density, acceleration
 
 

time: 102 us -> 101 us (level)
  waiting for transfers between devices: 11.6 us -> 9.71 us
  Pallas kernels: 16.9 us -> 18.3 us
    pallas_call x0 -> x1, Pallas kernels: none -> 1.94 us  [per_device(): pl.pallas_call(near_force_kernel, out_shape=shape(BINS, 3, SLOTS), in_spe...]
    all_to_all x1, waiting for transfers between devices: 6.64 us -> 4.71 us  [per_device(): inverse = lax.all_to_all(block, ('z', 'x'), 0, 0, tiled=True)]
  transfers between devices with their start and end apart: 7 -> 7, of which waited for: 3 -> 3; matrix products, arithmetic and copies ran while one was open for 0% -> 0% of each run, Pallas kernels for 8% -> 10%
where the time goes in v7:
time: 101 us; the launch traced here: 100 us
  starting transfers between devices  52.9 us (52%)
  Pallas kernels  18.3 us (18%)
  blocking collectives  18 us (18%)
  waiting for transfers between devices  9.71 us (10%)
    all_to_all x1, starting transfers between devices, per_device(): column = lax.all_to_all(block, 'z', 0, 0, tiled=True)  19.4 us
    all_to_all x1, blocking collectives, per_device(): lax.all_to_all(jnp.broadcast_to(column[None], (cols_count,) + column.shap...  13.6 us
    all_to_all x1, starting transfers between devices, per_device(): inverse = lax.all_to_all(block, ('z', 'x'), 0, 0, tiled=True)  13 us
    ppermute x4, starting transfers between devices, both_ways(): return (lax.ppermute(value, 'slab', up), lax.ppermute(value, 'slab', down))  12.3 us
    ppermute x1, starting transfers between devices, per_device(): far = lax.ppermute(near, 'core', [(0, 1), (1, 0)])  8.2 us
    ppermute x4, waiting for transfers between devices, both_ways(): return (lax.ppermute(value, 'slab', up), lax.ppermute(value, 'slab', down))  5 us
    all_to_all x1, waiting for transfers between devices, per_device(): inverse = lax.all_to_all(block, ('z', 'x'), 0, 0, tiled=True)  4.71 us
    all_gather x1, blocking collectives, per_device(): lax.all_gather(inverse.reshape(-1, SLOTS), 'core', axis=0, tiled=True)  4.45 us
  transfers between devices with their start and end apart: 7, of which 3 were waited for; matrix products, arithmetic and copies ran while one was open for 0% of the time, Pallas kernels for 10%

profile of v7, /device:TPU:1, one launch (start us, length us, event | category | flops | bytes accessed | tf_op | source)
XLA Modules:
  0.0 100.5 jit_solution(6653269990628201920)
XLA Ops:
  0.6 1.5 %prepare.1 = (f32[4,8,128]{2,1,0:T(8,128)}, f32[16,4,8,128]{3,2,1,0:T(8,128)}) custom-call(s32[4]{0:T(128)} %counts_in.1, f32[8,4,128]{2,1,0:T(4,128)} %particles_in.1), custom_call_target="tpu_custom_call" | custom-call | tf_op jit(solution)/shard_map/prepare/pallas_call | solution.py:255
  2.1 0.0 copy-start.2
  2.1 19.4 %all-to-all-start = ((f32[16,4,8,128]{3,2,1,0:T(8,128)}), f32[16,4,8,128]{3,2,1,0:T(8,128)S(1)}, u32[]{:S(2)}, u32[]{:S(2)}) async-start(f32[16,4,8,128]{3,2,1,0:T(8,128)} %get-tuple-element.23), calls=%async_computation | async-start | bytes 524288 | tf_op jit(solution)/shard_map/all_to_all | solution.py:269
  21.6 5.1 %collective-permute-start.1 = (f32[4,8,128]{2,1,0:T(8,128)}, f32[4,8,128]{2,1,0:T(8,128)S(1)}, u32[]{:S(2)}, u32[]{:S(2)}) collective-permute-start(f32[4,8,128]{2,1,0:T(8,128)} %get-tuple-element.22.own), channel_id=1, source_target_pairs={{128,0},{256,128},{384,256},{512,384},{640,512},{768,640},{896,768... | collective-permute-start | bytes 49160 | tf_op jit(solution)/shard_map/ppermute | solution.py:241
  26.7 1.9 %collective-permute-start = (f32[4,8,128]{2,1,0:T(8,128)}, f32[4,8,128]{2,1,0:T(8,128)S(1)}, u32[]{:S(2)}, u32[]{:S(2)}) collective-permute-start(f32[4,8,128]{2,1,0:T(8,128)} %get-tuple-element.22.own), channel_id=1, source_target_pairs={{0,128},{128,256},{256,384},{384,512},{512,640},{640,768},{768,896... | collective-permute-start | bytes 49160 | tf_op jit(solution)/shard_map/ppermute | solution.py:241
  28.6 4.3 %collective-permute-done.up = f32[4,8,128]{2,1,0:T(8,128)S(1)} collective-permute-done((f32[4,8,128]{2,1,0:T(8,128)}, f32[4,8,128]{2,1,0:T(8,128)S(1)}, u32[]{:S(2)}, u32[]{:S(2)}) %collective-permute-start) | collective-permute-done | bytes 16416 | tf_op jit(solution)/shard_map/ppermute | solution.py:241
  32.9 0.7 copy-done
  33.6 2.4 %near.1 = (f32[4,128]{1,0:T(4,128)S(1)}, f32[4,3,128,128]{3,2,1,0:T(8,128)S(1)}, f32[4,3,128]{2,1,0:T(4,128)S(1)}) custom-call(f32[4,8,128]{2,1,0:T(8,128)S(1)} %copy-done, f32[4,8,128]{2,1,0:T(8,128)S(1)} %collective-permute-done.up, f32[4,8,128]{2,1,0:T(8,128)S(1)} %collective-permute-done.1.down), custom_call_target="tpu_custom_call" | custom-call | flops 11796480 | bytes 786432 | tf_op jit(solution)/shard_map/near/pallas_call | solution.py:271
  36.0 0.0 all-to-all-done
  36.0 0.1 broadcast_in_dim.2
  36.1 13.6 %all_to_all.15 = f32[4,16,4,8,128]{4,3,2,1,0:T(8,128)S(1)} all-to-all(f32[4,16,4,8,128]{4,3,2,1,0:T(8,128)S(1)} %broadcast_in_dim.2), channel_id=1, replica_groups=mesh['slab'=8,'z'=16,'x'=4,'core'=2] {'x'}, dimensions={0} | all-to-all | bytes 2097152 | tf_op jit(solution)/shard_map/all_to_all | solution.py:282
  49.7 8.2 %collective-permute-start.2 = (f32[256,8,128]{2,1,0:T(8,128)S(1)}, f32[256,8,128]{2,1,0:T(8,128)S(1)}, u32[]{:S(2)}, u32[]{:S(2)}) collective-permute-start(f32[256,8,128]{2,1,0:T(8,128)S(1)} %bitcast.2), channel_id=1, source_target_pairs={{0,1},{1,0},{2,3},{3,2},{4,5},{5,4},{6,7},{7,6},{8,9},{9,8},{10,11... | collective-permute-start | bytes 3145736 | tf_op jit(solution)/shard_map/ppermute | solution.py:284
  57.9 2.7 %local_density.1 = (f32[4,4,128,128]{3,2,1,0:T(8,128)S(1)}, f32[4,128,128]{2,1,0:T(8,128)S(1)}) custom-call(s32[4,8]{1,0:T(4,128)S(1)} %copy-done.2, f32[4,8,128]{2,1,0:T(8,128)S(1)} %copy-done.1, f32[256,8,128]{2,1,0:T(8,128)S(1)} %bitcast.3), custom_call_target="tpu_custom_call" | custom-call | flops 10485760 | bytes 2097152 | tf_op jit(solution)/shard_map/local_density/pallas_call | solution.py:285
  60.6 0.0 collective-permute-done.2.far
  60.6 3.2 %partner_density.1 = (f32[4,128]{1,0:T(4,128)S(1)}, f32[4,128]{1,0:T(4,128)S(1)}, f32[64,4,128]{2,1,0:T(4,128)}, f32[32,8,128]{2,1,0:T(8,128)S(1)}) custom-call(s32[4,8]{1,0:T(4,128)S(1)} %copy-done.2, f32[4,8,128]{2,1,0:T(8,128)S(1)} %copy-done.1, f32[4,128]{1,0:T(4,128)S(1)} %get-tuple-element.27.part, f32[256,8,128]{2,1,0:T(8,128)S(1)} %bitcast.4, ...), custom_call_target="tpu_custom_call" | custom-call | flops 10485760 | bytes 2097152 | tf_op jit(solution)/shard_map/partner_density/pallas_call | solution.py:295
  63.8 13.0 %all-to-all-start.2 = ((f32[64,4,128]{2,1,0:T(4,128)}), f32[64,4,128]{2,1,0:T(4,128)S(1)}, u32[]{:S(2)}, u32[]{:S(2)}) async-start(f32[64,4,128]{2,1,0:T(4,128)} %get-tuple-element.35), calls=%async_computation.2 | async-start | bytes 262144 | tf_op jit(solution)/shard_map/all_to_all | solution.py:311
  76.8 3.3 %collective-permute-start.4 = (f32[4,128]{1,0:T(4,128)S(1)}, f32[4,128]{1,0:T(4,128)S(1)}, u32[]{:S(2)}, u32[]{:S(2)}) collective-permute-start(f32[4,128]{1,0:T(4,128)S(1)} %get-tuple-element.39.mine), channel_id=1, source_target_pairs={{128,0},{256,128},{384,256},{512,384},{640,512},{768,640},{896,768... | collective-permute-start | bytes 6152 | tf_op jit(solution)/shard_map/ppermute | solution.py:241
  80.1 2.0 %collective-permute-start.3 = (f32[4,128]{1,0:T(4,128)S(1)}, f32[4,128]{1,0:T(4,128)S(1)}, u32[]{:S(2)}, u32[]{:S(2)}) collective-permute-start(f32[4,128]{1,0:T(4,128)S(1)} %get-tuple-element.39.mine), channel_id=1, source_target_pairs={{0,128},{128,256},{256,384},{384,512},{512,640},{640,768},{768,896... | collective-permute-start | bytes 6152 | tf_op jit(solution)/shard_map/ppermute | solution.py:241
  82.1 3.1 %factor.1 = (f32[4,128]{1,0:T(4,128)}, f32[4,8,128,128]{3,2,1,0:T(8,128)S(1)}, f32[4,3,128]{2,1,0:T(4,128)S(1)}) custom-call(f32[4,8,128]{2,1,0:T(8,128)S(1)} %copy-done.1, f32[32,8,128]{2,1,0:T(8,128)S(1)} %get-tuple-element.31.members, f32[4,128]{1,0:T(4,128)S(1)} %get-tuple-element.32.density), custom_call_target="tpu_custom_call" | custom-call | flops 20971520 | bytes 2097152 | tf_op jit(solution)/shard_map/factor/pallas_call | solution.py:312
  85.2 0.7 collective-permute-done.3.mine_up
  85.9 1.9 %near_force.1.begun = f32[4,3,128]{2,1,0:T(4,128)S(1)} custom-call(f32[4,8,128]{2,1,0:T(8,128)S(1)} %copy-done.1, f32[4,8,128]{2,1,0:T(8,128)S(1)} %collective-permute-done.up, f32[4,8,128]{2,1,0:T(8,128)S(1)} %collective-permute-done.1.down, f32[4,3,128,128]{3,2,1,0:T(8,128)S(1)} %get-tuple-element.36.factors, ...), custom_call_target="tpu_custom_call" | custom-call | flops 7864320 | bytes 786432 | tf_op jit(solution)/shard_map/near_force/pallas_call | solution.py:327
  87.8 4.7 %all-to-all-done.2 = f32[64,4,128]{2,1,0:T(4,128)S(1)} async-done(((f32[64,4,128]{2,1,0:T(4,128)}), f32[64,4,128]{2,1,0:T(4,128)S(1)}, u32[]{:S(2)}, u32[]{:S(2)}) %all-to-all-start.2) | async-done | bytes 131104 | tf_op jit(solution)/shard_map/all_to_all | solution.py:311
  92.5 4.5 %all_gather.3.inverse = f32[512,128]{1,0:T(8,128)S(1)} all-gather(f32[256,128]{1,0:T(8,128)S(1)} %bitcast.5), channel_id=1, replica_groups=mesh['slab'=8,'z'=16,'x'=4,'core'=2] {'core'}, dimensions={0}, use_global_device_ids=true | all-gather | bytes 393216 | tf_op jit(solution)/shard_map/all_gather | solution.py:338
  97.0 3.5 %force.1 = f32[3,4,128]{2,1,0:T(4,128)} custom-call(s32[4,8]{1,0:T(4,128)S(1)} %copy-done.2, f32[4,8,128]{2,1,0:T(8,128)S(1)} %copy-done.1, f32[32,8,128]{2,1,0:T(8,128)S(1)} %get-tuple-element.31.members, f32[4,8,128,128]{3,2,1,0:T(8,128)S(1)} %get-tuple-element.34.factors, f32[4,3,128]{2,1,0:T(4,128)S(1)} %near_force.1.begun, ...), custom_call_target="tpu_custom_call" | custom-call | flops 10485760 | bytes 2097152 | tf_op jit(solution)/shard_map/force/pallas_call | solution.py:339
  (6 shorter events, 0.0 us)
Async XLA Ops:
  2.1 55.8 %copy-start.1 = (f32[4,8,128]{2,1,0:T(8,128)S(1)}, f32[4,8,128]{2,1,0:T(8,128)}, u32[]{:S(2)}) copy-start(f32[4,8,128]{2,1,0:T(8,128)} %get-tuple-element.22.own) | copy-start | bytes 49156
  2.1 55.8 %copy-start.2 = (s32[4,8]{1,0:T(4,128)S(1)}, s32[4,8]{1,0:T(4,128)}, u32[]{:S(2)}) copy-start(s32[4,8]{1,0:T(4,128)} %partners.5) | copy-start | bytes 388
  2.1 33.9 %all-to-all-start = ((f32[16,4,8,128]{3,2,1,0:T(8,128)}), f32[16,4,8,128]{3,2,1,0:T(8,128)S(1)}, u32[]{:S(2)}, u32[]{:S(2)}) async-start(f32[16,4,8,128]{3,2,1,0:T(8,128)} %get-tuple-element.23), calls=%async_computation | async-start | bytes 524288 | tf_op jit(solution)/shard_map/all_to_all | solution.py:269
  21.6 7.0 %collective-permute-start.1 = (f32[4,8,128]{2,1,0:T(8,128)}, f32[4,8,128]{2,1,0:T(8,128)S(1)}, u32[]{:S(2)}, u32[]{:S(2)}) collective-permute-start(f32[4,8,128]{2,1,0:T(8,128)} %get-tuple-element.22.own), channel_id=1, source_target_pairs={{128,0},{256,128},{384,256},{512,384},{640,512},{768,640},{896,768... | collective-permute-start | bytes 49160 | tf_op jit(solution)/shard_map/ppermute | solution.py:241
  26.7 6.2 %collective-permute-start = (f32[4,8,128]{2,1,0:T(8,128)}, f32[4,8,128]{2,1,0:T(8,128)S(1)}, u32[]{:S(2)}, u32[]{:S(2)}) collective-permute-start(f32[4,8,128]{2,1,0:T(8,128)} %get-tuple-element.22.own), channel_id=1, source_target_pairs={{0,128},{128,256},{256,384},{384,512},{512,640},{640,768},{768,896... | collective-permute-start | bytes 49160 | tf_op jit(solution)/shard_map/ppermute | solution.py:241
  32.9 0.7 copy-start
  49.7 10.9 %collective-permute-start.2 = (f32[256,8,128]{2,1,0:T(8,128)S(1)}, f32[256,8,128]{2,1,0:T(8,128)S(1)}, u32[]{:S(2)}, u32[]{:S(2)}) collective-permute-start(f32[256,8,128]{2,1,0:T(8,128)S(1)} %bitcast.2), channel_id=1, source_target_pairs={{0,1},{1,0},{2,3},{3,2},{4,5},{5,4},{6,7},{7,6},{8,9},{9,8},{10,11... | collective-permute-start | bytes 3145736 | tf_op jit(solution)/shard_map/ppermute | solution.py:284
  63.8 28.7 %all-to-all-start.2 = ((f32[64,4,128]{2,1,0:T(4,128)}), f32[64,4,128]{2,1,0:T(4,128)S(1)}, u32[]{:S(2)}, u32[]{:S(2)}) async-start(f32[64,4,128]{2,1,0:T(4,128)} %get-tuple-element.35), calls=%async_computation.2 | async-start | bytes 262144 | tf_op jit(solution)/shard_map/all_to_all | solution.py:311
  76.8 8.4 %collective-permute-start.4 = (f32[4,128]{1,0:T(4,128)S(1)}, f32[4,128]{1,0:T(4,128)S(1)}, u32[]{:S(2)}, u32[]{:S(2)}) collective-permute-start(f32[4,128]{1,0:T(4,128)S(1)} %get-tuple-element.39.mine), channel_id=1, source_target_pairs={{128,0},{256,128},{384,256},{512,384},{640,512},{768,640},{896,768... | collective-permute-start | bytes 6152 | tf_op jit(solution)/shard_map/ppermute | solution.py:241
  80.1 5.8 %collective-permute-start.3 = (f32[4,128]{1,0:T(4,128)S(1)}, f32[4,128]{1,0:T(4,128)S(1)}, u32[]{:S(2)}, u32[]{:S(2)}) collective-permute-start(f32[4,128]{1,0:T(4,128)S(1)} %get-tuple-element.39.mine), channel_id=1, source_target_pairs={{0,128},{128,256},{256,384},{384,512},{512,640},{640,768},{768,896... | collective-permute-start | bytes 6152 | tf_op jit(solution)/shard_map/ppermute | solution.py:241
